TPU v7x, 32 devices: a whole 2x2x4 slice. The times are simulated.
32 devices in a mesh: seq: 8 (over y, x, core), head: 4 (over z).
Axes of the slice: x: 2, y: 2, z: 4, core: 2. Of those that a mesh axis runs over, the one named last changes fastest.
Arguments:
- queries: bfloat16 [8192, 1024], P(('seq', 'head')), may hold values from -200 to 200
- keys: bfloat16 [8192, 512], P(('seq', 'head')), may hold values from -6.5 to 6.5
- values: bfloat16 [8192, 512], P(('seq', 'head')), may hold values from -6 to 6
- visible: int32 [8, 4], P('seq'), may hold values 0 or 1
Outputs:
- attended: bfloat16 [8192, 1024], P(('seq', 'head'))
All inputs are finite; a program needn't handle non-finite values. No bound on the sum of `visible` on one device may be relied on, other than what follows from the above.
Results may differ from a plain program's by a relative error of at most 0.0045.
Values may be sent and summed in bfloat16 or wider, within the bound.
No kernel may reach another device: no remote copies, remote signals or barrier semaphores. Data moves between devices by JAX's collectives and lax.ppermute only.
A program may use at most 128 MiB of HBM per device.

v0:
```python
import jax
import jax.numpy as jnp
from jax import lax
from jax.sharding import PartitionSpec as P

HEAD_SIZE = 128
QUERY_PER_KV = 2


attn_scale = 168.0 ** (-0.5)
powers = (1, 2, 4, 8)


def from_behind(shard, axis, by):
    count = lax.axis_size(axis)
    pairs = [(i, i + by) for i in range(count) if 0 <= i + by < count]
    return lax.ppermute(shard, axis, pairs)


def body(queries, keys, values, visible):
    query_loc, keys_loc, values_loc = (
        lax.all_to_all(queries, "head", split_axis=1, concat_axis=0, tiled=True),
        lax.all_to_all(keys, "head", split_axis=1, concat_axis=0, tiled=True),
        lax.all_to_all(values, "head", split_axis=1, concat_axis=0, tiled=True),
    )
    block_length = query_loc.shape[0]
    remote = [from_behind((keys_loc, values_loc), "seq", distance) for distance in powers]
    all_keys = jnp.concatenate([keys_loc] + [pair[0] for pair in remote], axis=0)
    all_values = jnp.concatenate([values_loc] + [pair[1] for pair in remote], axis=0)
    seq_index = lax.axis_index("seq")
    flag_arr = (visible[0] != 0) & (seq_index >= jnp.array(powers, jnp.int32))
    row_index = jnp.arange(block_length)[:, None]
    column = jnp.arange(5 * block_length)[None, :]
    region = column // block_length
    remote_ok = jnp.any(
        (region[None] == (jnp.arange(4) + 1)[:, None, None]) & flag_arr[:, None, None], axis=0
    )
    allowed = jnp.where(region == 0, column <= row_index, remote_ok)
    query_heads = query_loc.reshape(block_length, QUERY_PER_KV, HEAD_SIZE)
    outputs = []
    for member in range(QUERY_PER_KV):
        scores = (
            jnp.einsum(
                "qd,kd->qk", query_heads[:, member, :], all_keys, preferred_element_type=jnp.float32
            )
            * attn_scale
        )
        masked = jnp.where(allowed, scores, -1e30)
        peak = jnp.max(masked, axis=-1, keepdims=True)
        weights = jnp.where(allowed, jnp.exp(masked - peak), 0.0)
        total = jnp.sum(weights, axis=-1)
        rounded = weights.astype(jnp.bfloat16)
        numer = jnp.dot(rounded, all_values, preferred_element_type=jnp.float32)
        outputs.append((numer / total[:, None]).astype(jnp.bfloat16))
    merged = jnp.stack(outputs, axis=1).reshape(block_length, QUERY_PER_KV * HEAD_SIZE)
    return lax.all_to_all(merged, "head", split_axis=0, concat_axis=1, tiled=True)


def solution(mesh):
    return jax.shard_map(
        body,
        mesh=mesh,
        in_specs=(
            P(("seq", "head"), None),
            P(("seq", "head"), None),
            P(("seq", "head"), None),
            P("seq", None),
        ),
        out_specs=P(("seq", "head"), None),
        check_vma=False,
    )
```

profile of v0, /device:TPU:0, one launch (start us, length us, event | category | flops | bytes accessed | tf_op | source)
XLA Modules:
  0.0 135.6 jit_solution(2472858860828397660)
XLA Ops:
  0.0 1.8 %copy.19 = bf16[256,512]{0,1:T(8,128)(2,1)} copy(bf16[256,512]{1,0:T(8,128)(2,1)} %param.7) | data formatting | bytes 524288 | tf_op args[2]
  1.8 6.3 %all-to-all-start.2 = ((bf16[256,4,128]{0,2,1:T(8,128)(2,1)}), bf16[256,4,128]{0,2,1:T(8,128)(2,1)S(1)}, u32[]{:S(2)}, u32[]{:S(2)}) async-start(bf16[256,4,128]{0,2,1:T(8,128)(2,1)} %bitcast.6), calls=%async_computation.2 | async-start | bytes 524288 | tf_op jit(solution)/shard_map/all_to_all | solution.py:24
  8.1 1.8 %copy.16 = bf16[256,512]{0,1:T(8,128)(2,1)} copy(bf16[256,512]{1,0:T(8,128)(2,1)} %param.6) | data formatting | bytes 524288 | tf_op args[1]
  9.9 0.7 bitcast_and_fusion
  10.6 6.4 %all-to-all-done.2 = bf16[256,4,128]{0,2,1:T(8,128)(2,1)S(1)} async-done(((bf16[256,4,128]{0,2,1:T(8,128)(2,1)}), bf16[256,4,128]{0,2,1:T(8,128)(2,1)S(1)}, u32[]{:S(2)}, u32[]{:S(2)}) %all-to-all-start.2) | async-done | bytes 262176 | tf_op jit(solution)/shard_map/all_to_all | solution.py:24
  17.0 3.4 %all-to-all-start = ((bf16[256,4,128]{0,2,1:T(8,128)(2,1)}), bf16[256,4,128]{0,2,1:T(8,128)(2,1)S(1)}, u32[]{:S(2)}, u32[]{:S(2)}) async-start(bf16[256,4,128]{0,2,1:T(8,128)(2,1)} %bitcast.1), calls=%async_computation | async-start | bytes 524288 | tf_op jit(solution)/shard_map/all_to_all | solution.py:23
  20.5 0.1 and_reduce_fusion
  20.6 0.2 copy.20
  20.8 1.3 collective-permute-start.4
  22.1 1.9 %copy.38 = bf16[32,4,8,256]{3,2,0,1:T(8,128)(2,1)} copy(bf16[32,4,8,256]{3,2,1,0:T(8,128)(2,1)} %bitcast.68) | data formatting | bytes 1048576 | tf_op jit(solution)/shard_map/all_to_all | solution.py:22
  24.0 0.7 collective-permute-start.7
  24.6 4.1 %collective-permute-start.6 = (bf16[1024,128]{1,0:T(8,128)(2,1)S(1)}, bf16[1024,128]{1,0:T(8,128)(2,1)S(1)}, u32[]{:S(2)}, u32[]{:S(2)}) collective-permute-start(bf16[1024,128]{1,0:T(8,128)(2,1)S(1)} %bitcast.58), channel_id=1, source_target_pairs={{0,16},{4,20},{8,24},{12,28},{1,17},{5,21},{9,25},{13,29},{2,18},{... | collective-permute-start | bytes 786440 | tf_op jit(solution)/shard_map/ppermute | solution.py:17
  28.7 3.4 %collective-permute-start.5 = (bf16[1024,128]{1,0:T(8,128)(2,1)S(1)}, bf16[1024,128]{1,0:T(8,128)(2,1)S(1)}, u32[]{:S(2)}, u32[]{:S(2)}) collective-permute-start(bf16[1024,128]{1,0:T(8,128)(2,1)S(1)} %bitcast.59), channel_id=1, source_target_pairs={{0,8},{4,12},{8,16},{12,20},{16,24},{20,28},{1,9},{5,13},{9,17},{1... | collective-permute-start | bytes 786440 | tf_op jit(solution)/shard_map/ppermute | solution.py:17
  32.1 0.7 constant_dynamic-update-slice_fusion.9
  32.8 0.0 all-to-all-done
  32.8 5.1 %all-to-all-start.1 = ((bf16[256,4,256]{2,0,1:T(8,128)(2,1)}), bf16[256,4,256]{2,0,1:T(8,128)(2,1)S(1)}, u32[]{:S(2)}, u32[]{:S(2)}) async-start(bf16[256,4,256]{2,0,1:T(8,128)(2,1)} %bitcast.52), calls=%async_computation.1 | async-start | bytes 1048576 | tf_op jit(solution)/shard_map/all_to_all | solution.py:22
  37.9 0.2 copy.17
  38.1 0.7 collective-permute-start.3
  38.8 0.0 collective-permute-done.4
  38.8 1.3 collective-permute-start.2
  40.1 0.7 constant_dynamic-update-slice_fusion.8
  40.8 0.0 collective-permute-done.5
  40.8 1.4 %collective-permute-start = (bf16[1024,128]{1,0:T(8,128)(2,1)S(1)}, bf16[1024,128]{1,0:T(8,128)(2,1)S(1)}, u32[]{:S(2)}, u32[]{:S(2)}) collective-permute-start(bf16[1024,128]{1,0:T(8,128)(2,1)S(1)} %bitcast.64), channel_id=1, source_target_pairs={{0,4},{4,8},{8,12},{12,16},{16,20},{20,24},{24,28},{1,5},{5,9},{9,... | collective-permute-start | bytes 786440 | tf_op jit(solution)/shard_map/ppermute | solution.py:17
  42.3 0.7 constant_dynamic-update-slice_fusion.7
  43.0 0.0 collective-permute-done.6
  43.0 2.7 %collective-permute-start.1 = (bf16[1024,128]{1,0:T(8,128)(2,1)S(1)}, bf16[1024,128]{1,0:T(8,128)(2,1)S(1)}, u32[]{:S(2)}, u32[]{:S(2)}) collective-permute-start(bf16[1024,128]{1,0:T(8,128)(2,1)S(1)} %bitcast.65), channel_id=1, source_target_pairs={{0,8},{4,12},{8,16},{12,20},{16,24},{20,28},{1,9},{5,13},{9,17},{1... | collective-permute-start | bytes 786440 | tf_op jit(solution)/shard_map/ppermute | solution.py:17
  45.7 0.7 constant_dynamic-update-slice_fusion.6
  46.5 0.0 collective-permute-done.7
  46.5 0.7 constant_dynamic-update-slice_fusion.5
  47.2 0.0 collective-permute-done
  47.2 5.0 %collective-permute-done.1 = bf16[1024,128]{1,0:T(8,128)(2,1)S(1)} collective-permute-done((bf16[1024,128]{1,0:T(8,128)(2,1)S(1)}, bf16[1024,128]{1,0:T(8,128)(2,1)S(1)}, u32[]{:S(2)}, u32[]{:S(2)}) %collective-permute-start.1) | collective-permute-done | bytes 262176 | tf_op jit(solution)/shard_map/ppermute | solution.py:17
  52.3 2.8 %collective-permute-done.2 = bf16[1024,128]{1,0:T(8,128)(2,1)S(1)} collective-permute-done((bf16[1024,128]{1,0:T(8,128)(2,1)S(1)}, bf16[1024,128]{1,0:T(8,128)(2,1)S(1)}, u32[]{:S(2)}, u32[]{:S(2)}) %collective-permute-start.2) | collective-permute-done | bytes 262176 | tf_op jit(solution)/shard_map/ppermute | solution.py:17
  55.1 0.0 collective-permute-done.3
  55.1 0.0 all-to-all-done.1
  55.1 0.1 reshape.152
  55.3 0.7 fusion.36
  56.0 2.9 %fusion.25 = f32[5120,1024]{1,0:T(8,128)S(1)} fusion(bf16[5120,128]{1,0:T(8,128)(2,1)S(1)} %constant_dynamic-update-slice_fusion, bf16[1024,1,128]{2,1,0:T(2,128)(2,1)S(1)} %get-tuple-element.9), kind=kOutput, calls=%fused_computation.20 | convolution fusion | flops 1342177280 | bytes 22544384 | tf_op jit(solution)/shard_map/qd,kd->qk/dot_general | solution.py:43
  58.9 12.6 %fusion.1 = (f32[1024]{0:T(1024)S(1)}, f32[1024]{0:T(1024)S(1)}, f32[5120,1024]{1,0:T(8,128)}) fusion(pred[5120]{0:T(1024)(128)(4,1)S(1)} %and_reduce_fusion, pred[5120]{0:T(1024)(128)(4,1)S(1)} %broadcast_compare_fusion, f32[5120,1024]{1,0:T(8,128)S(1)} %fusion.25, bf16[5120,128]{1,0:T(8,128)(2,1)S(1)} %constant_dynamic-update-slice_fusion, ...), kind=kOutput, calls=%fused_computation.6 | convolution fusion | flops 1384118272 | bytes 43534336 | tf_op jit(solution)/shard_map/qd,kd->qk/dot_general | solution.py:43
  71.5 19.1 %fusion.34 = (f32[1024]{0:T(1024)S(1)}, f32[1024]{0:T(1024)S(1)}) fusion(f32[1024]{0:T(1024)S(1)} %get-tuple-element.7, f32[5120,1024]{1,0:T(8,128)} %get-tuple-element.11, pred[5120]{0:T(1024)(128)(4,1)S(1)} %and_reduce_fusion, pred[5120]{0:T(1024)(128)(4,1)S(1)} %broadcast_compare_fusion, f32[1024]{0:T(1024)S(1)} %get-tuple-element.8, ...), kind=kLoop, calls=%fused_computation.47 | loop fusion | flops 62912512 | bytes 41969664 | tf_op jit(solution)/shard_map/reduce_sum | solution.py:51
  90.7 0.0 copy-done
  90.7 7.1 %fusion.22 = bf16[1024,1,128]{2,0,1:T(8,128)(2,1)S(1)} fusion(bf16[5120,128]{1,0:T(8,128)(2,1)S(1)} %copy-done, f32[1024]{0:T(1024)S(1)} %get-tuple-element.6, f32[5120,1024]{1,0:T(8,128)S(1)} %fusion.25, f32[1024]{0:T(1024)S(1)} %get-tuple-element.8, pred[5120]{0:T(1024)(128)(4,1)S(1)} %and_reduce_fusion, pred[5120]{0:T(1024)(128)(4,1)S(1)} %broadcast_compare_fusion), kind=kOutput, calls=%fused_computation.17 | convolution fusion | flops 1379139584 | bytes 22562816 | tf_op jit(solution)/shard_map/dot_general | solution.py:53
  97.8 16.2 %fusion.13 = bf16[1024,1,128]{2,0,1:T(8,128)(2,1)S(1)} fusion(bf16[5120,128]{1,0:T(8,128)(2,1)S(1)} %copy-done, f32[1024]{0:T(1024)S(1)} %get-tuple-element.5, f32[5120,1024]{1,0:T(8,128)} %get-tuple-element.11, f32[1024]{0:T(1024)S(1)} %get-tuple-element.7, pred[5120]{0:T(1024)(128)(4,1)S(1)} %and_reduce_fusion, pred[5120]{0:T(1024)(128)(4,1)S(1)} %broadcast_compare_fusion), kind=kOutput, calls=%fused_computation.14 | convolution fusion | flops 1379139584 | bytes 22562816 | tf_op jit(solution)/shard_map/dot_general | solution.py:53
  114.0 0.1 pad_maximum_fusion
  114.1 0.5 copy.21
  114.6 0.3 all_to_all.65
  115.0 19.4 %all_to_all.73 = bf16[4,256,256]{2,1,0:T(8,128)(2,1)S(1)} all-to-all(bf16[4,256,256]{2,1,0:T(8,128)(2,1)S(1)} %all_to_all.65), channel_id=1, replica_groups=mesh['seq'=8,'head'=4] {'head'}, dimensions={0} | all-to-all | bytes 1048576 | tf_op jit(solution)/shard_map/all_to_all | solution.py:56
  134.4 0.2 copy.22
  134.6 1.0 copy.23
  (9 shorter events, 0.2 us)
Async XLA Ops:
  1.8 15.3 %all-to-all-start.2 = ((bf16[256,4,128]{0,2,1:T(8,128)(2,1)}), bf16[256,4,128]{0,2,1:T(8,128)(2,1)S(1)}, u32[]{:S(2)}, u32[]{:S(2)}) async-start(bf16[256,4,128]{0,2,1:T(8,128)(2,1)} %bitcast.6), calls=%async_computation.2 | async-start | bytes 524288 | tf_op jit(solution)/shard_map/all_to_all | solution.py:24
  17.0 15.8 %all-to-all-start = ((bf16[256,4,128]{0,2,1:T(8,128)(2,1)}), bf16[256,4,128]{0,2,1:T(8,128)(2,1)S(1)}, u32[]{:S(2)}, u32[]{:S(2)}) async-start(bf16[256,4,128]{0,2,1:T(8,128)(2,1)} %bitcast.1), calls=%async_computation | async-start | bytes 524288 | tf_op jit(solution)/shard_map/all_to_all | solution.py:23
  20.8 18.0 %collective-permute-start.4 = (bf16[1024,128]{1,0:T(8,128)(2,1)S(1)}, bf16[1024,128]{1,0:T(8,128)(2,1)S(1)}, u32[]{:S(2)}, u32[]{:S(2)}) collective-permute-start(bf16[1024,128]{1,0:T(8,128)(2,1)S(1)} %bitcast.56), channel_id=1, source_target_pairs={{0,4},{4,8},{8,12},{12,16},{16,20},{20,24},{24,28},{1,5},{5,9},{9,... | collective-permute-start | bytes 786440 | tf_op jit(solution)/shard_map/ppermute | solution.py:17
  24.0 22.5 %collective-permute-start.7 = (bf16[1024,128]{1,0:T(8,128)(2,1)S(1)}, bf16[1024,128]{1,0:T(8,128)(2,1)S(1)}, u32[]{:S(2)}, u32[]{:S(2)}) collective-permute-start(bf16[1024,128]{1,0:T(8,128)(2,1)S(1)} %bitcast.57), channel_id=1, source_target_pairs={} | collective-permute-start | bytes 786440 | tf_op jit(solution)/shard_map/ppermute | solution.py:17
  24.6 18.4 %collective-permute-start.6 = (bf16[1024,128]{1,0:T(8,128)(2,1)S(1)}, bf16[1024,128]{1,0:T(8,128)(2,1)S(1)}, u32[]{:S(2)}, u32[]{:S(2)}) collective-permute-start(bf16[1024,128]{1,0:T(8,128)(2,1)S(1)} %bitcast.58), channel_id=1, source_target_pairs={{0,16},{4,20},{8,24},{12,28},{1,17},{5,21},{9,25},{13,29},{2,18},{... | collective-permute-start | bytes 786440 | tf_op jit(solution)/shard_map/ppermute | solution.py:17
  28.7 12.1 %collective-permute-start.5 = (bf16[1024,128]{1,0:T(8,128)(2,1)S(1)}, bf16[1024,128]{1,0:T(8,128)(2,1)S(1)}, u32[]{:S(2)}, u32[]{:S(2)}) collective-permute-start(bf16[1024,128]{1,0:T(8,128)(2,1)S(1)} %bitcast.59), channel_id=1, source_target_pairs={{0,8},{4,12},{8,16},{12,20},{16,24},{20,28},{1,9},{5,13},{9,17},{1... | collective-permute-start | bytes 786440 | tf_op jit(solution)/shard_map/ppermute | solution.py:17
  32.8 22.3 %all-to-all-start.1 = ((bf16[256,4,256]{2,0,1:T(8,128)(2,1)}), bf16[256,4,256]{2,0,1:T(8,128)(2,1)S(1)}, u32[]{:S(2)}, u32[]{:S(2)}) async-start(bf16[256,4,256]{2,0,1:T(8,128)(2,1)} %bitcast.52), calls=%async_computation.1 | async-start | bytes 1048576 | tf_op jit(solution)/shard_map/all_to_all | solution.py:22
  38.1 17.0 %collective-permute-start.3 = (bf16[1024,128]{1,0:T(8,128)(2,1)S(1)}, bf16[1024,128]{1,0:T(8,128)(2,1)S(1)}, u32[]{:S(2)}, u32[]{:S(2)}) collective-permute-start(bf16[1024,128]{1,0:T(8,128)(2,1)S(1)} %bitcast.61), channel_id=1, source_target_pairs={} | collective-permute-start | bytes 786440 | tf_op jit(solution)/shard_map/ppermute | solution.py:17
  38.8 16.3 %collective-permute-start.2 = (bf16[1024,128]{1,0:T(8,128)(2,1)S(1)}, bf16[1024,128]{1,0:T(8,128)(2,1)S(1)}, u32[]{:S(2)}, u32[]{:S(2)}) collective-permute-start(bf16[1024,128]{1,0:T(8,128)(2,1)S(1)} %bitcast.63), channel_id=1, source_target_pairs={{0,16},{4,20},{8,24},{12,28},{1,17},{5,21},{9,25},{13,29},{2,18},{... | collective-permute-start | bytes 786440 | tf_op jit(solution)/shard_map/ppermute | solution.py:17
  40.8 6.4 %collective-permute-start = (bf16[1024,128]{1,0:T(8,128)(2,1)S(1)}, bf16[1024,128]{1,0:T(8,128)(2,1)S(1)}, u32[]{:S(2)}, u32[]{:S(2)}) collective-permute-start(bf16[1024,128]{1,0:T(8,128)(2,1)S(1)} %bitcast.64), channel_id=1, source_target_pairs={{0,4},{4,8},{8,12},{12,16},{16,20},{20,24},{24,28},{1,5},{5,9},{9,... | collective-permute-start | bytes 786440 | tf_op jit(solution)/shard_map/ppermute | solution.py:17
  43.0 9.2 %collective-permute-start.1 = (bf16[1024,128]{1,0:T(8,128)(2,1)S(1)}, bf16[1024,128]{1,0:T(8,128)(2,1)S(1)}, u32[]{:S(2)}, u32[]{:S(2)}) collective-permute-start(bf16[1024,128]{1,0:T(8,128)(2,1)S(1)} %bitcast.65), channel_id=1, source_target_pairs={{0,8},{4,12},{8,16},{12,20},{16,24},{20,28},{1,9},{5,13},{9,17},{1... | collective-permute-start | bytes 786440 | tf_op jit(solution)/shard_map/ppermute | solution.py:17
  71.5 19.1 %copy-start = (bf16[5120,128]{1,0:T(8,128)(2,1)S(1)}, bf16[5120,128]{1,0:T(8,128)(2,1)}, u32[]{:S(2)}) copy-start(bf16[5120,128]{1,0:T(8,128)(2,1)} %constant_dynamic-update-slice_fusion.5) | copy-start | bytes 3932164
where the time goes:
time: 136 us
  matrix products  38.8 us (29%)
  starting transfers between devices  30.4 us (22%)
  other arithmetic  20 us (15%)
  blocking collectives  19.4 us (14%)
  waiting for transfers between devices  14.2 us (10%)
  local copies, waits for them, and re-layouts  12.5 us (9%)
    dot_general x2, matrix products, body(): numer = jnp.dot(rounded, all_values, preferred_element_type=jnp.float32)  23.3 us
    all_to_all x1, blocking collectives, body(): lax.all_to_all(merged, 'head', split_axis=0, concat_axis=1, tiled=True)  19.4 us
    reduce_sum x1, other arithmetic, body(): total = jnp.sum(weights, axis=-1)  19.1 us
    ppermute x8, starting transfers between devices, from_behind(): return lax.ppermute(shard, axis, pairs)  15.6 us
    dot_general x2, matrix products, body(): jnp.einsum('qd,kd->qk', query_heads[:, member, :], all_keys, preferred_el...  15.5 us
    ppermute x8, waiting for transfers between devices, from_behind(): return lax.ppermute(shard, axis, pairs)  7.79 us
    unnamed x12, local copies, waits for them, and re-layouts  6.58 us
    all_to_all x1, waiting for transfers between devices, body(): lax.all_to_all(values, 'head', split_axis=1, concat_axis=0, tiled=True)  6.45 us
  transfers between devices with their start and end apart: 11, of which 3 were waited for; matrix products, arithmetic and copies ran while one was open for 6% of the time, Pallas kernels for 0%

commit v1 on v0

v1 whole, which is shorter than its diff:
```python
import math

import jax
import jax.numpy as jnp
from jax import lax
from jax.experimental import pallas as pl
from jax.experimental.pallas import tpu as pltpu
from jax.sharding import PartitionSpec as P

HEAD_SIZE = 128
QUERY_PER_KV = 2

attn_scale = 168.0 ** (-0.5)
log2_scale = attn_scale * math.log2(math.e)
powers = (1, 2, 4, 8)
NEG = -1e30
TILE = 256
CHUNK = 64
LANES = 128
CONTRACT_LAST = (((1,), (1,)), ((), ()))


def attend(visible, queries, members, slots, state, last):
    heads = lax.axis_size("head")
    tokens = queries.shape[0]
    share = tokens // heads
    tile = min(TILE, tokens)
    chunk = min(CHUNK, tile)
    begin = state is None
    n_state = 3

    def kernel(visible_ref, q_ref, *refs):
        refs = list(refs)
        take = lambda n: [refs.pop(0) for _ in range(n)]
        k_refs, v_refs = take(len(slots)), take(len(slots))
        if not begin:
            state_in = take(n_state)
        if last:
            (o_ref,) = take(1)
            state_out = state_in
        else:
            state_out = take(n_state)
        if begin:
            state_in = state_out
        score_refs, weight_refs = take(2), take(2)
        block = lax.axis_index("seq")
        place = lax.axis_index("head")
        seen = [
            None if d == 0 else (visible_ref[0, powers.index(d)] != 0) & (block >= d) for d, _, _ in slots
        ]

        def finish(base, numer, total):
            out = (numer / jnp.sum(total, axis=1, keepdims=True)).astype(o_ref.dtype)
            size = min(share, tile)
            for part in range(0, tile, size):
                start = base + part
                goes = lax.rem(lax.div(start, share) + heads - place, heads)
                inside = pl.ds(pl.multiple_of(lax.rem(start, share), size), size)
                o_ref[goes, inside, :] = out[part : part + size, :]

        def run(items, base):
            diagonal = base if isinstance(base, int) else None

            def score(i):
                member, slot, count, offset = items[i]
                columns = pl.ds(member * HEAD_SIZE, HEAD_SIZE)
                score_refs[i % 2][:, :count] = lax.dot_general(
                    q_ref[pl.ds(base + offset, tile), columns],
                    k_refs[slot][:count, :],
                    CONTRACT_LAST,
                    preferred_element_type=jnp.float32,
                )

            def soften(i):
                member, slot, count, offset = items[i]
                own = slots[slot][0] == 0
                fresh = begin and slot == 0
                for r in range(0, tile, chunk):
                    rows = pl.ds(base + offset + r, chunk)

                    def scores(j):
                        got = score_refs[i % 2][r : r + chunk, j : j + LANES]
                        if own and j + LANES > diagonal + r:
                            row = lax.broadcasted_iota(jnp.int32, got.shape, 0) + (diagonal + r - j)
                            column = lax.broadcasted_iota(jnp.int32, got.shape, 1)
                            got = jnp.where(column <= row, got, NEG)
                        return got

                    lanes = [j for j in range(0, count, LANES) if not (own and j >= diagonal + r + chunk)]
                    peak = scores(0)
                    for j in lanes[1:]:
                        peak = jnp.maximum(peak, scores(j))
                    peak = jnp.max(peak, axis=1, keepdims=True)
                    if not own:
                        peak = jnp.where(seen[slot], peak, NEG)
                    peak = jnp.broadcast_to(peak, (chunk, LANES))
                    if not fresh:
                        peak_ref, total_ref, numer_ref = (
                            state_in if slot == 0 else (peak_run, total_run, numer_run)
                        )
                        before = peak_ref[member, rows, :]
                        peak = jnp.maximum(before, peak)
                        shrink = jnp.exp2((before - peak) * log2_scale)
                    peak_run[member, rows, :] = peak
                    base_of = peak if own else jnp.where(seen[slot], peak, -NEG)
                    total = None
                    for j in range(0, count, LANES):
                        if j in lanes:
                            weights = jnp.exp2((scores(j) - base_of) * log2_scale)
                            total = weights if total is None else total + weights
                        else:
                            weights = jnp.zeros((chunk, LANES), jnp.float32)
                        weight_refs[i % 2][r : r + chunk, j : j + LANES] = weights.astype(jnp.bfloat16)
                    if not fresh:
                        total = total_ref[member, rows, :] * shrink + total
                        numer_run[member, rows, :] = numer_ref[member, rows, :] * shrink
                    total_run[member, rows, :] = total

            def mix(i):
                member, slot, count, offset = items[i]
                rows = pl.ds(base + offset, tile)
                numer = jnp.dot(
                    weight_refs[i % 2][:, :count], v_refs[slot][:count, :], preferred_element_type=jnp.float32
                )
                if not (begin and slot == 0):
                    numer = numer_run[member, rows, :] + numer
                if last and slot == len(slots) - 1:
                    finish(base + offset, numer, total_run[member, rows, :])
                else:
                    numer_run[member, rows, :] = numer

            score(0)
            for i in range(len(items)):
                if i + 1 < len(items):
                    score(i + 1)
                if i > 0 and items[i - 1][::3] == items[i][::3]:
                    mix(i - 1)
                    soften(i)
                else:
                    soften(i)
                    if i > 0:
                        mix(i - 1)
            mix(len(items) - 1)

        if last:
            peak_run, total_run, numer_run = take(3)
        else:
            peak_run, total_run, numer_run = state_out

        if slots[0][0] == 0:
            for start in range(0, tokens, tile):
                run([(m, 0, start + tile, 0) for m in members], start)
        else:

            group = 2 * tile if tokens % (2 * tile) == 0 else tile
            order = [
                (m, slot, tokens, offset)
                for slot in range(len(slots))
                for offset in range(0, group, tile)
                for m in members
            ]

            @pl.loop(0, tokens // group)
            def _(step):
                run(order, pl.multiple_of(step * group, group))

    vmem = pl.BlockSpec(memory_space=pltpu.VMEM)
    pairs = tokens * tokens * len(slots) * len(members)
    whole = jax.ShapeDtypeStruct((QUERY_PER_KV, tokens, LANES), jnp.float32)
    scratch = [pltpu.VMEM((tile, tokens), jnp.float32)] * 2 + [pltpu.VMEM((tile, tokens), jnp.bfloat16)] * 2
    if last:
        out_shape = jax.ShapeDtypeStruct((heads, share, HEAD_SIZE), queries.dtype)
        scratch += [pltpu.VMEM(whole.shape, jnp.float32)] * 3
    else:
        out_shape = [whole] * n_state
    operands = [visible, queries] + [k for _, k, _ in slots] + [v for _, _, v in slots] + list(state or ())
    aliases = {}
    if not begin and not last:
        aliases = {len(operands) - n_state + i: i for i in range(n_state)}
    return pl.pallas_call(
        kernel,
        out_shape=out_shape,
        in_specs=[pl.BlockSpec(memory_space=pltpu.SMEM)] + [vmem] * (len(operands) - 1),
        out_specs=vmem if last else [vmem] * n_state,
        scratch_shapes=scratch,
        input_output_aliases=aliases,
        cost_estimate=pl.CostEstimate(
            flops=4 * pairs * HEAD_SIZE, transcendentals=pairs, bytes_accessed=8 * tokens * HEAD_SIZE * len(slots)
        ),
        compiler_params=pltpu.CompilerParams(vmem_limit_bytes=14 << 20),
    )(*operands)


def split_by_head(arrays):
    heads = lax.axis_size("head")
    share = arrays[0].shape[0]
    widths = [array.shape[1] // heads for array in arrays]

    def kernel(*refs):
        place = lax.axis_index("head")
        sems = refs[-1]
        copies = []
        for i, width in enumerate(widths):
            for j in range(heads):
                start = pl.multiple_of(lax.rem(place + j, heads) * width, HEAD_SIZE)
                at = i * heads + j
                copies.append(
                    pltpu.make_async_copy(refs[i].at[:, pl.ds(start, width)], refs[len(widths) + at], sems.at[at])
                )
        for copy in copies:
            copy.start()
        for copy in copies:
            copy.wait()

    vmem = pl.BlockSpec(memory_space=pltpu.VMEM)
    pieces = pl.pallas_call(
        kernel,
        out_shape=[
            jax.ShapeDtypeStruct((share, width), arrays[0].dtype) for width in widths for _ in range(heads)
        ],
        in_specs=[pl.BlockSpec(memory_space=pltpu.HBM)] * len(widths),
        out_specs=[vmem] * (heads * len(widths)),
        scratch_shapes=[pltpu.SemaphoreType.DMA((heads * len(widths),))],
        compiler_params=pltpu.CompilerParams(vmem_limit_bytes=8 << 20),
    )(*arrays)
    return [pieces[i * heads : (i + 1) * heads] for i in range(len(widths))]


def join_heads(pieces):
    heads = lax.axis_size("head")
    share, width = pieces[0][0].shape

    def kernel(*refs):
        place = lax.axis_index("head")
        out_ref = refs[-1]
        ins = iter(refs)
        for member in range(len(pieces)):
            for j in range(heads):
                source = lax.rem(place + heads - j, heads)
                start = pl.multiple_of((source * len(pieces) + member) * width, HEAD_SIZE)
                out_ref[:, pl.ds(start, width)] = next(ins)[...]

    vmem = pl.BlockSpec(memory_space=pltpu.VMEM)
    flat = [piece for group in pieces for piece in group]
    return pl.pallas_call(
        kernel,
        out_shape=jax.ShapeDtypeStruct((share, heads * len(pieces) * width), flat[0].dtype),
        in_specs=[vmem] * len(flat),
        out_specs=vmem,
        compiler_params=pltpu.CompilerParams(vmem_limit_bytes=8 << 20),
    )(*flat)


def body(queries, keys, values, visible):
    heads = lax.axis_size("head")
    blocks = lax.axis_size("seq")
    place = lax.axis_index("head")
    block = lax.axis_index("seq")
    share = queries.shape[0]
    tokens = share * heads

    def rotate(piece, by):
        return lax.ppermute(piece, "head", [(i, (i + by) % heads) for i in range(heads)])

    def gather_tokens(pieces):
        got = [piece if j == 0 else rotate(piece, j) for j, piece in enumerate(pieces)]
        whole = jnp.zeros((tokens, pieces[0].shape[1]), pieces[0].dtype)
        for j in range(heads):
            source = lax.rem(place + heads - j, heads)
            whole = lax.dynamic_update_slice(whole, got[j], (source * share, 0))
        return whole

    def move(array, pairs):
        return lax.ppermute(array, "seq", [p for p in pairs if 0 <= min(p) and max(p) < blocks])

    distances = tuple(d for d in powers if d < blocks)
    relayed = [b for b in range(4, blocks - 2) if b & 3 == 1]

    def behind(own):
        far = {}
        for d in distances:
            if d > 2:
                far[d] = move(own, [(b - d, b) for b in range(d, blocks)])
        got = dict(far)
        if 2 in distances:
            got[2] = move(own, [(b - 2, b) for b in range(2, blocks) if b not in relayed])
            if relayed:
                through = move(far[4], [(b + 2, b) for b in relayed])
                is_relayed = (block >= 4) & (block < blocks - 2) & (block & 3 == 1)
                got[2] = jnp.where(is_relayed, through, got[2])
        if 1 in distances:
            if 2 in distances and blocks % 2 == 0:
                out = jnp.where(block % 2 == 0, own, got[2])
                got[1] = move(out, [(b, b ^ 1) for b in range(blocks)])
            else:
                got[1] = move(own, [(b - 1, b) for b in range(1, blocks)])
        return got

    (key_parts,) = split_by_head([keys])
    (value_parts, query_parts) = split_by_head([values, queries])
    key_own = gather_tokens(key_parts)
    key_behind = behind(key_own)
    value_own = gather_tokens(value_parts)
    value_behind = behind(value_own)
    query_own = gather_tokens(query_parts)
    members = list(range(QUERY_PER_KV))
    far = [(d, key_behind[d], value_behind[d]) for d in reversed(distances) if d > 2]
    near = [(d, key_behind[d], value_behind[d]) for d in reversed(distances) if d <= 2]
    state = attend(visible, query_own, members, [(0, key_own, value_own)], None, False)
    if far:
        state = attend(visible, query_own, members, far, state, False)
    pieces = []
    for member in members:
        out = attend(visible, query_own, [member], near, state, True)
        pieces.append([out[0]] + [rotate(out[j], j) for j in range(1, heads)])
    return join_heads(pieces)


def solution(mesh):
    return jax.shard_map(
        body,
        mesh=mesh,
        in_specs=(
            P(("seq", "head"), None),
            P(("seq", "head"), None),
            P(("seq", "head"), None),
            P("seq", None),
        ),
        out_specs=P(("seq", "head"), None),
        check_vma=False,
    )
```

time: 136 us -> 73.7 us (0.54)
  matrix products: 38.8 us -> 0 us
  other arithmetic: 20 us -> 0.1 us
  blocking collectives: 19.4 us -> 0 us
  Pallas kernels: 0 us -> 18.1 us
  local copies, waits for them, and re-layouts: 12.5 us -> 2.88 us
  starting transfers between devices: 30.4 us -> 39.7 us
  waiting for transfers between devices: 14.2 us -> 12.3 us
    dot_general x4 -> x0, matrix products: 38.8 us -> none  [the longest x2 23.3 us: body(): numer = jnp.dot(rounded, all_values, preferred_element_type=jnp.float32)]
    ppermute x8 -> x23, starting transfers between devices: 15.6 us -> 39.7 us  [the longest x15 24.3 us: rotate(): lax.ppermute(piece, 'head', [(i, (i + by) % heads) for i in range(heads)])]
    all_to_all x1 -> x0, blocking collectives: 19.4 us -> none  [body(): lax.all_to_all(merged, 'head', split_axis=0, concat_axis=1, tiled=True)]
    reduce_sum x1 -> x0, other arithmetic: 19.1 us -> none  [body(): total = jnp.sum(weights, axis=-1)]
    pallas_call x0 -> x7, Pallas kernels: none -> 18.1 us  [the longest x4 16.8 us: attend(): pl.pallas_call(kernel, out_shape=out_shape, in_specs=[pl.BlockSpec(memory...]
    all_to_all x3 -> x0, starting transfers between devices: 14.8 us -> none  [the longest x1 6.35 us: body(): lax.all_to_all(values, 'head', split_axis=1, concat_axis=0, tiled=True)]
    all_to_all x3 -> x0, waiting for transfers between devices: 6.45 us -> none  [the longest x1 6.45 us: body(): lax.all_to_all(values, 'head', split_axis=1, concat_axis=0, tiled=True)]
    ppermute x8 -> x23, waiting for transfers between devices: 7.79 us -> 12.3 us  [the longest x15 7.56 us: rotate(): lax.ppermute(piece, 'head', [(i, (i + by) % heads) for i in range(heads)])]
  transfers between devices with their start and end apart: 11 -> 23, of which waited for: 3 -> 5; matrix products, arithmetic and copies ran while one was open for 6% -> 1% of each run, Pallas kernels for 0% -> 17%
where the time goes in v1:
time: 73.7 us; the launch traced here: 73.4 us
  starting transfers between devices  39.7 us (54%)
  Pallas kernels  18.1 us (25%)
  waiting for transfers between devices  12.3 us (17%)
  local copies, waits for them, and re-layouts  2.88 us (4%)
    ppermute x15, starting transfers between devices, rotate(): lax.ppermute(piece, 'head', [(i, (i + by) % heads) for i in range(heads)])  24.3 us
    pallas_call x4, Pallas kernels, attend(): pl.pallas_call(kernel, out_shape=out_shape, in_specs=[pl.BlockSpec(memory...  16.8 us
    ppermute x8, starting transfers between devices, move(): lax.ppermute(array, 'seq', [p for p in pairs if 0 <= min(p) and max(p) <...  15.3 us
    ppermute x15, waiting for transfers between devices, rotate(): lax.ppermute(piece, 'head', [(i, (i + by) % heads) for i in range(heads)])  7.56 us
    ppermute x8, waiting for transfers between devices, move(): lax.ppermute(array, 'seq', [p for p in pairs if 0 <= min(p) and max(p) <...  4.76 us
    unnamed x8, local copies, waits for them, and re-layouts  2.53 us
  transfers between devices with their start and end apart: 23, of which 5 were waited for; matrix products, arithmetic and copies ran while one was open for 1% of the time, Pallas kernels for 17%

profile of v1, /device:TPU:0, one launch (start us, length us, event | category | flops | bytes accessed | tf_op | source)
XLA Modules:
  0.0 73.4 jit_solution(5830749353824504575)
XLA Ops:
  0.0 1.0 %copy-done = bf16[256,1024]{1,0:T(8,128)(2,1)S(1)} copy-done((bf16[256,1024]{1,0:T(8,128)(2,1)S(1)}, bf16[256,1024]{1,0:T(8,128)(2,1)}, u32[]{:S(2)}) %copy-start) | copy-done | bytes 524312
  1.0 0.9 %copy-done.1 = bf16[256,512]{1,0:T(8,128)(2,1)S(1)} copy-done((bf16[256,512]{1,0:T(8,128)(2,1)S(1)}, bf16[256,512]{1,0:T(8,128)(2,1)}, u32[]{:S(2)}) %copy-start.1) | copy-done | bytes 262168
  2.0 0.2 shard_map.46
  2.2 3.1 %collective-permute-start.10 = (bf16[256,128]{1,0:T(8,128)(2,1)S(1)}, bf16[256,128]{1,0:T(8,128)(2,1)S(1)}, u32[]{:S(2)}, u32[]{:S(2)}) collective-permute-start(bf16[256,128]{1,0:T(8,128)(2,1)S(1)} %get-tuple-element.32), channel_id=1, source_target_pairs={{0,1},{1,2},{2,3},{3,0},{4,5},{5,6},{6,7},{7,4},{8,9},{9,10},{10,1... | collective-permute-start | bytes 196616 | tf_op jit(solution)/shard_map/ppermute | solution.py:263
  5.3 2.6 %collective-permute-start.11 = (bf16[256,128]{1,0:T(8,128)(2,1)S(1)}, bf16[256,128]{1,0:T(8,128)(2,1)S(1)}, u32[]{:S(2)}, u32[]{:S(2)}) collective-permute-start(bf16[256,128]{1,0:T(8,128)(2,1)S(1)} %get-tuple-element.33), channel_id=1, source_target_pairs={{0,2},{1,3},{2,0},{3,1},{4,6},{5,7},{6,4},{7,5},{8,10},{9,11},{10,... | collective-permute-start | bytes 196616 | tf_op jit(solution)/shard_map/ppermute | solution.py:263
  7.9 1.3 %collective-permute-start.12 = (bf16[256,128]{1,0:T(8,128)(2,1)S(1)}, bf16[256,128]{1,0:T(8,128)(2,1)S(1)}, u32[]{:S(2)}, u32[]{:S(2)}) collective-permute-start(bf16[256,128]{1,0:T(8,128)(2,1)S(1)} %get-tuple-element.34), channel_id=1, source_target_pairs={{0,3},{1,0},{2,1},{3,2},{4,7},{5,4},{6,5},{7,6},{8,11},{9,8},{10,9... | collective-permute-start | bytes 196616 | tf_op jit(solution)/shard_map/ppermute | solution.py:263
  9.3 0.1 shard_map.47
  9.4 0.7 collective-permute-start.3
  10.1 0.3 collective-permute-start.4
  10.6 2.9 %collective-permute-start.5 = (bf16[256,128]{1,0:T(8,128)(2,1)S(1)}, bf16[256,128]{1,0:T(8,128)(2,1)S(1)}, u32[]{:S(2)}, u32[]{:S(2)}) collective-permute-start(bf16[256,128]{1,0:T(8,128)(2,1)S(1)} %get-tuple-element.30), channel_id=1, source_target_pairs={{0,3},{1,0},{2,1},{3,2},{4,7},{5,4},{6,5},{7,6},{8,11},{9,8},{10,9... | collective-permute-start | bytes 196616 | tf_op jit(solution)/shard_map/ppermute | solution.py:263
  13.4 0.0 collective-permute-done.11
  13.5 0.0 collective-permute-done.12
  13.5 3.4 %collective-permute-start.13 = (bf16[1024,128]{1,0:T(8,128)(2,1)S(1)}, bf16[1024,128]{1,0:T(8,128)(2,1)S(1)}, u32[]{:S(2)}, u32[]{:S(2)}) collective-permute-start(bf16[1024,128]{1,0:T(8,128)(2,1)S(1)} %constant_dynamic-update-slice_fusion.refs_1_), channel_id=1, source_target_pairs={{0,16},{4,20},{8,24},{12,28},{1,17},{5,21},{9,25},{13,29},{2,18},{... | collective-permute-start | bytes 786440 | tf_op jit(solution)/shard_map/ppermute | solution.py:274
  17.0 0.0 collective-permute-done.3
  17.0 1.0 %collective-permute-done.4 = bf16[256,128]{1,0:T(8,128)(2,1)S(1)} collective-permute-done((bf16[256,128]{1,0:T(8,128)(2,1)S(1)}, bf16[256,128]{1,0:T(8,128)(2,1)S(1)}, u32[]{:S(2)}, u32[]{:S(2)}) %collective-permute-start.4) | collective-permute-done | bytes 65568 | tf_op jit(solution)/shard_map/ppermute | solution.py:263
  18.0 0.0 collective-permute-done.5
  18.1 3.7 %collective-permute-start.6 = (bf16[1024,128]{1,0:T(8,128)(2,1)S(1)}, bf16[1024,128]{1,0:T(8,128)(2,1)S(1)}, u32[]{:S(2)}, u32[]{:S(2)}) collective-permute-start(bf16[1024,128]{1,0:T(8,128)(2,1)S(1)} %constant_dynamic-update-slice_fusion.4.refs_0_), channel_id=1, source_target_pairs={{0,16},{4,20},{8,24},{12,28},{1,17},{5,21},{9,25},{13,29},{2,18},{... | collective-permute-start | bytes 786440 | tf_op jit(solution)/shard_map/ppermute | solution.py:274
  21.7 1.6 %collective-permute-start = (bf16[256,256]{1,0:T(8,128)(2,1)S(1)}, bf16[256,256]{1,0:T(8,128)(2,1)S(1)}, u32[]{:S(2)}, u32[]{:S(2)}) collective-permute-start(bf16[256,256]{1,0:T(8,128)(2,1)S(1)} %get-tuple-element.24), channel_id=1, source_target_pairs={{0,1},{1,2},{2,3},{3,0},{4,5},{5,6},{6,7},{7,4},{8,9},{9,10},{10,1... | collective-permute-start | bytes 393224 | tf_op jit(solution)/shard_map/ppermute | solution.py:263
  23.3 2.0 %collective-permute-start.1 = (bf16[256,256]{1,0:T(8,128)(2,1)S(1)}, bf16[256,256]{1,0:T(8,128)(2,1)S(1)}, u32[]{:S(2)}, u32[]{:S(2)}) collective-permute-start(bf16[256,256]{1,0:T(8,128)(2,1)S(1)} %get-tuple-element.25), channel_id=1, source_target_pairs={{0,2},{1,3},{2,0},{3,1},{4,6},{5,7},{6,4},{7,5},{8,10},{9,11},{10,... | collective-permute-start | bytes 393224 | tf_op jit(solution)/shard_map/ppermute | solution.py:263
  25.4 3.4 %collective-permute-start.15 = (bf16[1024,128]{1,0:T(8,128)(2,1)S(1)}, bf16[1024,128]{1,0:T(8,128)(2,1)S(1)}, u32[]{:S(2)}, u32[]{:S(2)}) collective-permute-start(bf16[1024,128]{1,0:T(8,128)(2,1)S(1)} %constant_dynamic-update-slice_fusion.refs_1_), channel_id=1, source_target_pairs={{0,8},{4,12},{8,16},{16,24},{20,28},{1,9},{5,13},{9,17},{17,25},{2... | collective-permute-start | bytes 786440 | tf_op jit(solution)/shard_map/ppermute | solution.py:274
  28.8 0.0 collective-permute-done.13.refs_1_
  28.8 0.7 collective-permute-start.14
  29.6 0.8 %collective-permute-start.2 = (bf16[256,256]{1,0:T(8,128)(2,1)S(1)}, bf16[256,256]{1,0:T(8,128)(2,1)S(1)}, u32[]{:S(2)}, u32[]{:S(2)}) collective-permute-start(bf16[256,256]{1,0:T(8,128)(2,1)S(1)} %get-tuple-element.26), channel_id=1, source_target_pairs={{0,3},{1,0},{2,1},{3,2},{4,7},{5,4},{6,5},{7,6},{8,11},{9,8},{10,9... | collective-permute-start | bytes 393224 | tf_op jit(solution)/shard_map/ppermute | solution.py:263
  30.5 3.4 %collective-permute-done.1 = bf16[256,256]{1,0:T(8,128)(2,1)S(1)} collective-permute-done((bf16[256,256]{1,0:T(8,128)(2,1)S(1)}, bf16[256,256]{1,0:T(8,128)(2,1)S(1)}, u32[]{:S(2)}, u32[]{:S(2)}) %collective-permute-start.1) | collective-permute-done | bytes 131104 | tf_op jit(solution)/shard_map/ppermute | solution.py:263
  33.8 3.4 %collective-permute-start.8 = (bf16[1024,128]{1,0:T(8,128)(2,1)S(1)}, bf16[1024,128]{1,0:T(8,128)(2,1)S(1)}, u32[]{:S(2)}, u32[]{:S(2)}) collective-permute-start(bf16[1024,128]{1,0:T(8,128)(2,1)S(1)} %constant_dynamic-update-slice_fusion.4.refs_0_), channel_id=1, source_target_pairs={{0,8},{4,12},{8,16},{16,24},{20,28},{1,9},{5,13},{9,17},{17,25},{2... | collective-permute-start | bytes 786440 | tf_op jit(solution)/shard_map/ppermute | solution.py:274
  37.2 0.7 collective-permute-start.7
  37.9 0.0 collective-permute-done.14
  38.0 0.1 collective-permute-start.16
  38.1 4.7 %collective-permute-done.8 = bf16[1024,128]{1,0:T(8,128)(2,1)S(1)} collective-permute-done((bf16[1024,128]{1,0:T(8,128)(2,1)S(1)}, bf16[1024,128]{1,0:T(8,128)(2,1)S(1)}, u32[]{:S(2)}, u32[]{:S(2)}) %collective-permute-start.8) | collective-permute-done | bytes 262176 | tf_op jit(solution)/shard_map/ppermute | solution.py:274
  42.8 0.0 collective-permute-done.7
  42.8 0.1 broadcast_select_fusion.1
  42.9 0.0 copy-start.3
  42.9 0.1 collective-permute-start.9
  43.0 0.0 collective-permute-done.2
  43.0 0.5 copy-done.3
  43.5 2.9 %shard_map.48 = (f32[2,1024,128]{2,1,0:T(8,128)S(1)}, f32[2,1024,128]{2,1,0:T(8,128)S(1)}, f32[2,1024,128]{2,1,0:T(8,128)S(1)}) custom-call(s32[1,4]{1,0:T(1,128)S(1)} %copy-done.3, bf16[1024,256]{1,0:T(8,128)(2,1)S(1)} %constant_dynamic-update-slice_fusion.8.q_ref, bf16[1024,128]{1,0:T(8,128)(2,1)S(1)} %constant_dynamic-update-slice_fusion.4.refs_0_, ...), custom_call_target="tpu_custom_call" | custom-call | flops 1073741824 | bytes 1048576 | tf_op jit(solution)/shard_map/pallas_call | solution.py:180
  46.5 4.5 %shard_map.49 = (f32[2,1024,128]{2,1,0:T(8,128)S(1)}, f32[2,1024,128]{2,1,0:T(8,128)S(1)}, f32[2,1024,128]{2,1,0:T(8,128)S(1)}) custom-call(s32[1,4]{1,0:T(1,128)S(1)} %copy-done.3, bf16[1024,256]{1,0:T(8,128)(2,1)S(1)} %constant_dynamic-update-slice_fusion.8.q_ref, ...), custom_call_target="tpu_custom_call", output_to_operand_aliasing={{0}: (4, {}), {1}: (5, {}), {2}: (6, {})} | custom-call | flops 1073741824 | bytes 1048576 | tf_op jit(solution)/shard_map/pallas_call | solution.py:180
  51.0 4.7 %shard_map.51 = bf16[4,256,128]{2,1,0:T(8,128)(2,1)S(1)} custom-call(s32[1,4]{1,0:T(1,128)S(1)} %copy-done.3, bf16[1024,256]{1,0:T(8,128)(2,1)S(1)} %constant_dynamic-update-slice_fusion.8.q_ref, bf16[1024,128]{1,0:T(8,128)(2,1)S(1)} %get-tuple-element.44.refs_0_, bf16[1024,128]{1,0:T(8,128)(2,1)S(1)} %collective-permute-done.9.refs_1_, ...), custom_call_target="tpu_custom_call" | custom-call | flops 1073741824 | bytes 2097152 | tf_op jit(solution)/shard_map/pallas_call | solution.py:180
  55.8 0.1 collective-permute-start.20
  55.8 2.6 %collective-permute-start.21 = (bf16[256,128]{1,0:T(8,128)(2,1)S(1)}, bf16[256,128]{1,0:T(8,128)(2,1)S(1)}, u32[]{:S(2)}, u32[]{:S(2)}) collective-permute-start(bf16[256,128]{1,0:T(8,128)(2,1)S(1)} %get-tuple-element.46), channel_id=1, source_target_pairs={{0,2},{1,3},{2,0},{3,1},{4,6},{5,7},{6,4},{7,5},{8,10},{9,11},{10,... | collective-permute-start | bytes 196616 | tf_op jit(solution)/shard_map/ppermute | solution.py:263
  58.4 1.2 %collective-permute-start.22 = (bf16[256,128]{1,0:T(8,128)(2,1)S(1)}, bf16[256,128]{1,0:T(8,128)(2,1)S(1)}, u32[]{:S(2)}, u32[]{:S(2)}) collective-permute-start(bf16[256,128]{1,0:T(8,128)(2,1)S(1)} %get-tuple-element.45), channel_id=1, source_target_pairs={{0,3},{1,0},{2,1},{3,2},{4,7},{5,4},{6,5},{7,6},{8,11},{9,8},{10,9... | collective-permute-start | bytes 196616 | tf_op jit(solution)/shard_map/ppermute | solution.py:263
  59.6 4.7 %shard_map.50 = bf16[4,256,128]{2,1,0:T(8,128)(2,1)S(1)} custom-call(s32[1,4]{1,0:T(1,128)S(1)} %copy-done.3, bf16[1024,256]{1,0:T(8,128)(2,1)S(1)} %constant_dynamic-update-slice_fusion.8.q_ref, bf16[1024,128]{1,0:T(8,128)(2,1)S(1)} %get-tuple-element.44.refs_0_, bf16[1024,128]{1,0:T(8,128)(2,1)S(1)} %collective-permute-done.9.refs_1_, ...), custom_call_target="tpu_custom_call" | custom-call | flops 1073741824 | bytes 2097152 | tf_op jit(solution)/shard_map/pallas_call | solution.py:180
  64.4 0.8 %collective-permute-start.17 = (bf16[256,128]{1,0:T(8,128)(2,1)S(1)}, bf16[256,128]{1,0:T(8,128)(2,1)S(1)}, u32[]{:S(2)}, u32[]{:S(2)}) collective-permute-start(bf16[256,128]{1,0:T(8,128)(2,1)S(1)} %get-tuple-element.51), channel_id=1, source_target_pairs={{0,1},{1,2},{2,3},{3,0},{4,5},{5,6},{6,7},{7,4},{8,9},{9,10},{10,1... | collective-permute-start | bytes 196616 | tf_op jit(solution)/shard_map/ppermute | solution.py:263
  65.2 1.3 %collective-permute-start.18 = (bf16[256,128]{1,0:T(8,128)(2,1)S(1)}, bf16[256,128]{1,0:T(8,128)(2,1)S(1)}, u32[]{:S(2)}, u32[]{:S(2)}) collective-permute-start(bf16[256,128]{1,0:T(8,128)(2,1)S(1)} %get-tuple-element.50), channel_id=1, source_target_pairs={{0,2},{1,3},{2,0},{3,1},{4,6},{5,7},{6,4},{7,5},{8,10},{9,11},{10,... | collective-permute-start | bytes 196616 | tf_op jit(solution)/shard_map/ppermute | solution.py:263
  66.5 2.8 %collective-permute-start.19 = (bf16[256,128]{1,0:T(8,128)(2,1)S(1)}, bf16[256,128]{1,0:T(8,128)(2,1)S(1)}, u32[]{:S(2)}, u32[]{:S(2)}) collective-permute-start(bf16[256,128]{1,0:T(8,128)(2,1)S(1)} %get-tuple-element.49), channel_id=1, source_target_pairs={{0,3},{1,0},{2,1},{3,2},{4,7},{5,4},{6,5},{7,6},{8,11},{9,8},{10,9... | collective-permute-start | bytes 196616 | tf_op jit(solution)/shard_map/ppermute | solution.py:263
  69.4 1.7 %collective-permute-done.17.refs_1_ = bf16[256,128]{1,0:T(8,128)(2,1)S(1)} collective-permute-done((bf16[256,128]{1,0:T(8,128)(2,1)S(1)}, bf16[256,128]{1,0:T(8,128)(2,1)S(1)}, u32[]{:S(2)}, u32[]{:S(2)}) %collective-permute-start.17) | collective-permute-done | bytes 65568 | tf_op jit(solution)/shard_map/ppermute | solution.py:263
  71.0 1.5 %collective-permute-done.18.refs_2_ = bf16[256,128]{1,0:T(8,128)(2,1)S(1)} collective-permute-done((bf16[256,128]{1,0:T(8,128)(2,1)S(1)}, bf16[256,128]{1,0:T(8,128)(2,1)S(1)}, u32[]{:S(2)}, u32[]{:S(2)}) %collective-permute-start.18) | collective-permute-done | bytes 65568 | tf_op jit(solution)/shard_map/ppermute | solution.py:263
  72.5 0.9 %shard_map.52 = bf16[256,1024]{1,0:T(8,128)(2,1)} custom-call(bf16[256,128]{1,0:T(8,128)(2,1)S(1)} %get-tuple-element.52.refs_0_, bf16[256,128]{1,0:T(8,128)(2,1)S(1)} %collective-permute-done.17.refs_1_, bf16[256,128]{1,0:T(8,128)(2,1)S(1)} %collective-permute-done.18.refs_2_, bf16[256,128]{1,0:T(8,128)(2,1)S(1)} %collective-permute-done.19.refs_3_, ...), custom_call_target="tpu_custom_call" | custom-call | tf_op jit(solution)/shard_map/pallas_call | solution.py:245
  (32 shorter events, 0.4 us)
Async XLA Ops:
  0.0 1.0 %copy-start = (bf16[256,1024]{1,0:T(8,128)(2,1)S(1)}, bf16[256,1024]{1,0:T(8,128)(2,1)}, u32[]{:S(2)}) copy-start(bf16[256,1024]{1,0:T(8,128)(2,1)} %refs_1_.1) | copy-start | bytes 1572868
  1.0 0.9 %copy-start.1 = (bf16[256,512]{1,0:T(8,128)(2,1)S(1)}, bf16[256,512]{1,0:T(8,128)(2,1)}, u32[]{:S(2)}) copy-start(bf16[256,512]{1,0:T(8,128)(2,1)} %refs_0_.2) | copy-start | bytes 786436
  2.0 7.3 %copy-start.2 = (bf16[256,512]{1,0:T(8,128)(2,1)S(1)}, bf16[256,512]{1,0:T(8,128)(2,1)}, u32[]{:S(2)}) copy-start(bf16[256,512]{1,0:T(8,128)(2,1)} %refs_0_.3) | copy-start | bytes 786436
  2.2 8.3 %collective-permute-start.10 = (bf16[256,128]{1,0:T(8,128)(2,1)S(1)}, bf16[256,128]{1,0:T(8,128)(2,1)S(1)}, u32[]{:S(2)}, u32[]{:S(2)}) collective-permute-start(bf16[256,128]{1,0:T(8,128)(2,1)S(1)} %get-tuple-element.32), channel_id=1, source_target_pairs={{0,1},{1,2},{2,3},{3,0},{4,5},{5,6},{6,7},{7,4},{8,9},{9,10},{10,1... | collective-permute-start | bytes 196616 | tf_op jit(solution)/shard_map/ppermute | solution.py:263
  5.3 8.1 %collective-permute-start.11 = (bf16[256,128]{1,0:T(8,128)(2,1)S(1)}, bf16[256,128]{1,0:T(8,128)(2,1)S(1)}, u32[]{:S(2)}, u32[]{:S(2)}) collective-permute-start(bf16[256,128]{1,0:T(8,128)(2,1)S(1)} %get-tuple-element.33), channel_id=1, source_target_pairs={{0,2},{1,3},{2,0},{3,1},{4,6},{5,7},{6,4},{7,5},{8,10},{9,11},{10,... | collective-permute-start | bytes 196616 | tf_op jit(solution)/shard_map/ppermute | solution.py:263
  7.9 5.6 %collective-permute-start.12 = (bf16[256,128]{1,0:T(8,128)(2,1)S(1)}, bf16[256,128]{1,0:T(8,128)(2,1)S(1)}, u32[]{:S(2)}, u32[]{:S(2)}) collective-permute-start(bf16[256,128]{1,0:T(8,128)(2,1)S(1)} %get-tuple-element.34), channel_id=1, source_target_pairs={{0,3},{1,0},{2,1},{3,2},{4,7},{5,4},{6,5},{7,6},{8,11},{9,8},{10,9... | collective-permute-start | bytes 196616 | tf_op jit(solution)/shard_map/ppermute | solution.py:263
  9.4 7.6 %collective-permute-start.3 = (bf16[256,128]{1,0:T(8,128)(2,1)S(1)}, bf16[256,128]{1,0:T(8,128)(2,1)S(1)}, u32[]{:S(2)}, u32[]{:S(2)}) collective-permute-start(bf16[256,128]{1,0:T(8,128)(2,1)S(1)} %get-tuple-element.28), channel_id=1, source_target_pairs={{0,1},{1,2},{2,3},{3,0},{4,5},{5,6},{6,7},{7,4},{8,9},{9,10},{10,1... | collective-permute-start | bytes 196616 | tf_op jit(solution)/shard_map/ppermute | solution.py:263
  10.1 7.9 %collective-permute-start.4 = (bf16[256,128]{1,0:T(8,128)(2,1)S(1)}, bf16[256,128]{1,0:T(8,128)(2,1)S(1)}, u32[]{:S(2)}, u32[]{:S(2)}) collective-permute-start(bf16[256,128]{1,0:T(8,128)(2,1)S(1)} %get-tuple-element.29), channel_id=1, source_target_pairs={{0,2},{1,3},{2,0},{3,1},{4,6},{5,7},{6,4},{7,5},{8,10},{9,11},{10,... | collective-permute-start | bytes 196616 | tf_op jit(solution)/shard_map/ppermute | solution.py:263
  10.6 7.5 %collective-permute-start.5 = (bf16[256,128]{1,0:T(8,128)(2,1)S(1)}, bf16[256,128]{1,0:T(8,128)(2,1)S(1)}, u32[]{:S(2)}, u32[]{:S(2)}) collective-permute-start(bf16[256,128]{1,0:T(8,128)(2,1)S(1)} %get-tuple-element.30), channel_id=1, source_target_pairs={{0,3},{1,0},{2,1},{3,2},{4,7},{5,4},{6,5},{7,6},{8,11},{9,8},{10,9... | collective-permute-start | bytes 196616 | tf_op jit(solution)/shard_map/ppermute | solution.py:263
  13.5 15.3 %collective-permute-start.13 = (bf16[1024,128]{1,0:T(8,128)(2,1)S(1)}, bf16[1024,128]{1,0:T(8,128)(2,1)S(1)}, u32[]{:S(2)}, u32[]{:S(2)}) collective-permute-start(bf16[1024,128]{1,0:T(8,128)(2,1)S(1)} %constant_dynamic-update-slice_fusion.refs_1_), channel_id=1, source_target_pairs={{0,16},{4,20},{8,24},{12,28},{1,17},{5,21},{9,25},{13,29},{2,18},{... | collective-permute-start | bytes 786440 | tf_op jit(solution)/shard_map/ppermute | solution.py:274
  18.1 19.1 %collective-permute-start.6 = (bf16[1024,128]{1,0:T(8,128)(2,1)S(1)}, bf16[1024,128]{1,0:T(8,128)(2,1)S(1)}, u32[]{:S(2)}, u32[]{:S(2)}) collective-permute-start(bf16[1024,128]{1,0:T(8,128)(2,1)S(1)} %constant_dynamic-update-slice_fusion.4.refs_0_), channel_id=1, source_target_pairs={{0,16},{4,20},{8,24},{12,28},{1,17},{5,21},{9,25},{13,29},{2,18},{... | collective-permute-start | bytes 786440 | tf_op jit(solution)/shard_map/ppermute | solution.py:274
  21.7 7.9 %collective-permute-start = (bf16[256,256]{1,0:T(8,128)(2,1)S(1)}, bf16[256,256]{1,0:T(8,128)(2,1)S(1)}, u32[]{:S(2)}, u32[]{:S(2)}) collective-permute-start(bf16[256,256]{1,0:T(8,128)(2,1)S(1)} %get-tuple-element.24), channel_id=1, source_target_pairs={{0,1},{1,2},{2,3},{3,0},{4,5},{5,6},{6,7},{7,4},{8,9},{9,10},{10,1... | collective-permute-start | bytes 393224 | tf_op jit(solution)/shard_map/ppermute | solution.py:263
  23.3 10.5 %collective-permute-start.1 = (bf16[256,256]{1,0:T(8,128)(2,1)S(1)}, bf16[256,256]{1,0:T(8,128)(2,1)S(1)}, u32[]{:S(2)}, u32[]{:S(2)}) collective-permute-start(bf16[256,256]{1,0:T(8,128)(2,1)S(1)} %get-tuple-element.25), channel_id=1, source_target_pairs={{0,2},{1,3},{2,0},{3,1},{4,6},{5,7},{6,4},{7,5},{8,10},{9,11},{10,... | collective-permute-start | bytes 393224 | tf_op jit(solution)/shard_map/ppermute | solution.py:263
  25.4 12.5 %collective-permute-start.15 = (bf16[1024,128]{1,0:T(8,128)(2,1)S(1)}, bf16[1024,128]{1,0:T(8,128)(2,1)S(1)}, u32[]{:S(2)}, u32[]{:S(2)}) collective-permute-start(bf16[1024,128]{1,0:T(8,128)(2,1)S(1)} %constant_dynamic-update-slice_fusion.refs_1_), channel_id=1, source_target_pairs={{0,8},{4,12},{8,16},{16,24},{20,28},{1,9},{5,13},{9,17},{17,25},{2... | collective-permute-start | bytes 786440 | tf_op jit(solution)/shard_map/ppermute | solution.py:274
  28.8 9.1 %collective-permute-start.14 = (bf16[1024,128]{1,0:T(8,128)(2,1)S(1)}, bf16[1024,128]{1,0:T(8,128)(2,1)S(1)}, u32[]{:S(2)}, u32[]{:S(2)}) collective-permute-start(bf16[1024,128]{1,0:T(8,128)(2,1)S(1)} %collective-permute-done.13.refs_1_), channel_id=1, source_target_pairs={{28,20},{29,21},{30,22},{31,23}} | collective-permute-start | bytes 786440 | tf_op jit(solution)/shard_map/ppermute | solution.py:274
  29.6 13.4 %collective-permute-start.2 = (bf16[256,256]{1,0:T(8,128)(2,1)S(1)}, bf16[256,256]{1,0:T(8,128)(2,1)S(1)}, u32[]{:S(2)}, u32[]{:S(2)}) collective-permute-start(bf16[256,256]{1,0:T(8,128)(2,1)S(1)} %get-tuple-element.26), channel_id=1, source_target_pairs={{0,3},{1,0},{2,1},{3,2},{4,7},{5,4},{6,5},{7,6},{8,11},{9,8},{10,9... | collective-permute-start | bytes 393224 | tf_op jit(solution)/shard_map/ppermute | solution.py:263
  33.8 9.0 %collective-permute-start.8 = (bf16[1024,128]{1,0:T(8,128)(2,1)S(1)}, bf16[1024,128]{1,0:T(8,128)(2,1)S(1)}, u32[]{:S(2)}, u32[]{:S(2)}) collective-permute-start(bf16[1024,128]{1,0:T(8,128)(2,1)S(1)} %constant_dynamic-update-slice_fusion.4.refs_0_), channel_id=1, source_target_pairs={{0,8},{4,12},{8,16},{16,24},{20,28},{1,9},{5,13},{9,17},{17,25},{2... | collective-permute-start | bytes 786440 | tf_op jit(solution)/shard_map/ppermute | solution.py:274
  37.2 5.6 %collective-permute-start.7 = (bf16[1024,128]{1,0:T(8,128)(2,1)S(1)}, bf16[1024,128]{1,0:T(8,128)(2,1)S(1)}, u32[]{:S(2)}, u32[]{:S(2)}) collective-permute-start(bf16[1024,128]{1,0:T(8,128)(2,1)S(1)} %collective-permute-done.6.refs_0_), channel_id=1, source_target_pairs={{28,20},{29,21},{30,22},{31,23}} | collective-permute-start | bytes 786440 | tf_op jit(solution)/shard_map/ppermute | solution.py:274
  38.0 13.0 %collective-permute-start.16 = (bf16[1024,128]{1,0:T(8,128)(2,1)S(1)}, bf16[1024,128]{1,0:T(8,128)(2,1)S(1)}, u32[]{:S(2)}, u32[]{:S(2)}) collective-permute-start(bf16[1024,128]{1,0:T(8,128)(2,1)S(1)} %get-tuple-element.41), channel_id=1, source_target_pairs={{0,4},{4,0},{8,12},{12,8},{16,20},{20,16},{24,28},{28,24},{1,5},{5... | collective-permute-start | bytes 786440 | tf_op jit(solution)/shard_map/ppermute | solution.py:274
  42.9 0.7 copy-start.3
  42.9 8.1 %collective-permute-start.9 = (bf16[1024,128]{1,0:T(8,128)(2,1)S(1)}, bf16[1024,128]{1,0:T(8,128)(2,1)S(1)}, u32[]{:S(2)}, u32[]{:S(2)}) collective-permute-start(bf16[1024,128]{1,0:T(8,128)(2,1)S(1)} %get-tuple-element.43), channel_id=1, source_target_pairs={{0,4},{4,0},{8,12},{12,8},{16,20},{20,16},{24,28},{28,24},{1,5},{5... | collective-permute-start | bytes 786440 | tf_op jit(solution)/shard_map/ppermute | solution.py:274
  55.8 10.7 %collective-permute-start.20 = (bf16[256,128]{1,0:T(8,128)(2,1)S(1)}, bf16[256,128]{1,0:T(8,128)(2,1)S(1)}, u32[]{:S(2)}, u32[]{:S(2)}) collective-permute-start(bf16[256,128]{1,0:T(8,128)(2,1)S(1)} %get-tuple-element.47), channel_id=1, source_target_pairs={{0,1},{1,2},{2,3},{3,0},{4,5},{5,6},{6,7},{7,4},{8,9},{9,10},{10,1... | collective-permute-start | bytes 196616 | tf_op jit(solution)/shard_map/ppermute | solution.py:263
  55.8 13.5 %collective-permute-start.21 = (bf16[256,128]{1,0:T(8,128)(2,1)S(1)}, bf16[256,128]{1,0:T(8,128)(2,1)S(1)}, u32[]{:S(2)}, u32[]{:S(2)}) collective-permute-start(bf16[256,128]{1,0:T(8,128)(2,1)S(1)} %get-tuple-element.46), channel_id=1, source_target_pairs={{0,2},{1,3},{2,0},{3,1},{4,6},{5,7},{6,4},{7,5},{8,10},{9,11},{10,... | collective-permute-start | bytes 196616 | tf_op jit(solution)/shard_map/ppermute | solution.py:263
  58.4 11.0 %collective-permute-start.22 = (bf16[256,128]{1,0:T(8,128)(2,1)S(1)}, bf16[256,128]{1,0:T(8,128)(2,1)S(1)}, u32[]{:S(2)}, u32[]{:S(2)}) collective-permute-start(bf16[256,128]{1,0:T(8,128)(2,1)S(1)} %get-tuple-element.45), channel_id=1, source_target_pairs={{0,3},{1,0},{2,1},{3,2},{4,7},{5,4},{6,5},{7,6},{8,11},{9,8},{10,9... | collective-permute-start | bytes 196616 | tf_op jit(solution)/shard_map/ppermute | solution.py:263
  64.4 6.7 %collective-permute-start.17 = (bf16[256,128]{1,0:T(8,128)(2,1)S(1)}, bf16[256,128]{1,0:T(8,128)(2,1)S(1)}, u32[]{:S(2)}, u32[]{:S(2)}) collective-permute-start(bf16[256,128]{1,0:T(8,128)(2,1)S(1)} %get-tuple-element.51), channel_id=1, source_target_pairs={{0,1},{1,2},{2,3},{3,0},{4,5},{5,6},{6,7},{7,4},{8,9},{9,10},{10,1... | collective-permute-start | bytes 196616 | tf_op jit(solution)/shard_map/ppermute | solution.py:263
  65.2 7.3 %collective-permute-start.18 = (bf16[256,128]{1,0:T(8,128)(2,1)S(1)}, bf16[256,128]{1,0:T(8,128)(2,1)S(1)}, u32[]{:S(2)}, u32[]{:S(2)}) collective-permute-start(bf16[256,128]{1,0:T(8,128)(2,1)S(1)} %get-tuple-element.50), channel_id=1, source_target_pairs={{0,2},{1,3},{2,0},{3,1},{4,6},{5,7},{6,4},{7,5},{8,10},{9,11},{10,... | collective-permute-start | bytes 196616 | tf_op jit(solution)/shard_map/ppermute | solution.py:263
  66.5 6.0 %collective-permute-start.19 = (bf16[256,128]{1,0:T(8,128)(2,1)S(1)}, bf16[256,128]{1,0:T(8,128)(2,1)S(1)}, u32[]{:S(2)}, u32[]{:S(2)}) collective-permute-start(bf16[256,128]{1,0:T(8,128)(2,1)S(1)} %get-tuple-element.49), channel_id=1, source_target_pairs={{0,3},{1,0},{2,1},{3,2},{4,7},{5,4},{6,5},{7,6},{8,11},{9,8},{10,9... | collective-permute-start | bytes 196616 | tf_op jit(solution)/shard_map/ppermute | solution.py:263

commit v2 on v1

--- a/solution.py
+++ b/solution.py
@@ -20,13 +20,14 @@
 CONTRACT_LAST = (((1,), (1,)), ((), ()))
 
 
-def attend(visible, queries, members, slots, state, last):
+def attend(visible, queries, members, slots, state, last, goes=None):
     heads = lax.axis_size("head")
     tokens = queries.shape[0]
     share = tokens // heads
     tile = min(TILE, tokens)
     chunk = min(CHUNK, tile)
     begin = state is None
+    by_goal = goes is not None
     n_state = 3
 
     def kernel(visible_ref, q_ref, *refs):
@@ -49,34 +50,47 @@
             None if d == 0 else (visible_ref[0, powers.index(d)] != 0) & (block >= d) for d, _, _ in slots
         ]
 
-        def finish(base, numer, total):
+        if by_goal:
+            offsets = [
+                pl.multiple_of(lax.rem(place + j, heads) * share + sub, tile)
+                for j in goes
+                for sub in range(0, share, tile)
+            ]
+        else:
+            offsets = list(range(0, tokens, tile))
+
+        def finish(number, base, numer, total):
             out = (numer / jnp.sum(total, axis=1, keepdims=True)).astype(o_ref.dtype)
+            if by_goal:
+                each = share // tile
+                o_ref[number // each, pl.ds(number % each * tile, tile), :] = out
+                return
             size = min(share, tile)
             for part in range(0, tile, size):
                 start = base + part
-                goes = lax.rem(lax.div(start, share) + heads - place, heads)
-                inside = pl.ds(pl.multiple_of(lax.rem(start, share), size), size)
-                o_ref[goes, inside, :] = out[part : part + size, :]
-
-        def run(items, base):
-            diagonal = base if isinstance(base, int) else None
+                goal = lax.rem(start // share + heads - place, heads)
+                o_ref[goal, pl.ds(start % share, size), :] = out[part : part + size, :]
+
+        def run(items):
+            at = lambda i: offsets[items[i][3]]
 
             def score(i):
-                member, slot, count, offset = items[i]
+                member, slot, count, _ = items[i]
                 columns = pl.ds(member * HEAD_SIZE, HEAD_SIZE)
                 score_refs[i % 2][:, :count] = lax.dot_general(
-                    q_ref[pl.ds(base + offset, tile), columns],
+                    q_ref[pl.ds(at(i), tile), columns],
                     k_refs[slot][:count, :],
                     CONTRACT_LAST,
                     preferred_element_type=jnp.float32,
                 )
 
             def soften(i):
-                member, slot, count, offset = items[i]
+                member, slot, count, _ = items[i]
                 own = slots[slot][0] == 0
                 fresh = begin and slot == 0
+                diagonal = at(i)
                 for r in range(0, tile, chunk):
-                    rows = pl.ds(base + offset + r, chunk)
+                    rows = pl.ds(at(i) + r, chunk)
 
                     def scores(j):
                         got = score_refs[i % 2][r : r + chunk, j : j + LANES]
@@ -117,15 +131,15 @@
                     total_run[member, rows, :] = total
 
             def mix(i):
-                member, slot, count, offset = items[i]
-                rows = pl.ds(base + offset, tile)
+                member, slot, count, number = items[i]
+                rows = pl.ds(at(i), tile)
                 numer = jnp.dot(
                     weight_refs[i % 2][:, :count], v_refs[slot][:count, :], preferred_element_type=jnp.float32
                 )
                 if not (begin and slot == 0):
                     numer = numer_run[member, rows, :] + numer
                 if last and slot == len(slots) - 1:
-                    finish(base + offset, numer, total_run[member, rows, :])
+                    finish(number, at(i), numer, total_run[member, rows, :])
                 else:
                     numer_run[member, rows, :] = numer
 
@@ -147,29 +161,21 @@
         else:
             peak_run, total_run, numer_run = state_out
 
-        if slots[0][0] == 0:
-            for start in range(0, tokens, tile):
-                run([(m, 0, start + tile, 0) for m in members], start)
-        else:
-
-            group = 2 * tile if tokens % (2 * tile) == 0 else tile
-            order = [
-                (m, slot, tokens, offset)
+        run(
+            [
+                (m, slot, tokens if slots[slot][0] else (number + 1) * tile, number)
                 for slot in range(len(slots))
-                for offset in range(0, group, tile)
+                for number in range(len(offsets))
                 for m in members
             ]
-
-            @pl.loop(0, tokens // group)
-            def _(step):
-                run(order, pl.multiple_of(step * group, group))
+        )
 
     vmem = pl.BlockSpec(memory_space=pltpu.VMEM)
     pairs = tokens * tokens * len(slots) * len(members)
     whole = jax.ShapeDtypeStruct((QUERY_PER_KV, tokens, LANES), jnp.float32)
     scratch = [pltpu.VMEM((tile, tokens), jnp.float32)] * 2 + [pltpu.VMEM((tile, tokens), jnp.bfloat16)] * 2
     if last:
-        out_shape = jax.ShapeDtypeStruct((heads, share, HEAD_SIZE), queries.dtype)
+        out_shape = jax.ShapeDtypeStruct((len(goes) if by_goal else heads, share, HEAD_SIZE), queries.dtype)
         scratch += [pltpu.VMEM(whole.shape, jnp.float32)] * 3
     else:
         out_shape = [whole] * n_state
@@ -310,9 +316,18 @@
     if far:
         state = attend(visible, query_own, members, far, state, False)
     pieces = []
+    tile = min(TILE, tokens)
     for member in members:
-        out = attend(visible, query_own, [member], near, state, True)
-        pieces.append([out[0]] + [rotate(out[j], j) for j in range(1, heads)])
+        groups = [None]
+        if member == members[-1] and share % tile == 0 and heads > 2:
+            cut = heads // 2 + 1
+            groups = [list(range(1, cut)), list(range(cut, heads)) + [0]]
+        got = {}
+        for goes in groups:
+            out = attend(visible, query_own, [member], near, state, True, goes)
+            for i, j in enumerate(goes or range(heads)):
+                got[j] = rotate(out[i], j) if j else out[i]
+        pieces.append([got[j] for j in range(heads)])
     return join_heads(pieces)
 
 

time: 73.7 us -> 73.7 us (level)
    pallas_call x4 -> x5, Pallas kernels: 16.8 us -> 16.6 us  [attend(): pl.pallas_call(kernel, out_shape=out_shape, in_specs=[pl.BlockSpec(memory...]
  transfers between devices with their start and end apart: 23 -> 23, of which waited for: 5 -> 5; matrix products, arithmetic and copies ran while one was open for 1% -> 1% of each run, Pallas kernels for 17% -> 19%
where the time goes in v2:
time: 73.7 us; the launch traced here: 73.5 us
  starting transfers between devices  39.9 us (54%)
  Pallas kernels  17.9 us (24%)
  waiting for transfers between devices  12.3 us (17%)
  local copies, waits for them, and re-layouts  2.88 us (4%)
    ppermute x15, starting transfers between devices, rotate(): lax.ppermute(piece, 'head', [(i, (i + by) % heads) for i in range(heads)])  24.6 us
    pallas_call x5, Pallas kernels, attend(): pl.pallas_call(kernel, out_shape=out_shape, in_specs=[pl.BlockSpec(memory...  16.6 us
    ppermute x8, starting transfers between devices, move(): lax.ppermute(array, 'seq', [p for p in pairs if 0 <= min(p) and max(p) <...  15.3 us
    ppermute x15, waiting for transfers between devices, rotate(): lax.ppermute(piece, 'head', [(i, (i + by) % heads) for i in range(heads)])  7.54 us
    ppermute x8, waiting for transfers between devices, move(): lax.ppermute(array, 'seq', [p for p in pairs if 0 <= min(p) and max(p) <...  4.76 us
    unnamed x8, local copies, waits for them, and re-layouts  2.53 us
  transfers between devices with their start and end apart: 23, of which 5 were waited for; matrix products, arithmetic and copies ran while one was open for 1% of the time, Pallas kernels for 19%

profile of v2, /device:TPU:0, one launch (start us, length us, event | category | flops | bytes accessed | tf_op | source)
XLA Modules:
  0.0 73.5 jit_solution(3254524971777133252)
XLA Ops:
  0.0 1.0 %copy-done = bf16[256,1024]{1,0:T(8,128)(2,1)S(1)} copy-done((bf16[256,1024]{1,0:T(8,128)(2,1)S(1)}, bf16[256,1024]{1,0:T(8,128)(2,1)}, u32[]{:S(2)}) %copy-start) | copy-done | bytes 524312
  1.0 0.9 %copy-done.1 = bf16[256,512]{1,0:T(8,128)(2,1)S(1)} copy-done((bf16[256,512]{1,0:T(8,128)(2,1)S(1)}, bf16[256,512]{1,0:T(8,128)(2,1)}, u32[]{:S(2)}) %copy-start.1) | copy-done | bytes 262168
  2.0 0.2 shard_map.46
  2.2 3.1 %collective-permute-start.10 = (bf16[256,128]{1,0:T(8,128)(2,1)S(1)}, bf16[256,128]{1,0:T(8,128)(2,1)S(1)}, u32[]{:S(2)}, u32[]{:S(2)}) collective-permute-start(bf16[256,128]{1,0:T(8,128)(2,1)S(1)} %get-tuple-element.32), channel_id=1, source_target_pairs={{0,1},{1,2},{2,3},{3,0},{4,5},{5,6},{6,7},{7,4},{8,9},{9,10},{10,1... | collective-permute-start | bytes 196616 | tf_op jit(solution)/shard_map/ppermute | solution.py:269
  5.3 2.6 %collective-permute-start.11 = (bf16[256,128]{1,0:T(8,128)(2,1)S(1)}, bf16[256,128]{1,0:T(8,128)(2,1)S(1)}, u32[]{:S(2)}, u32[]{:S(2)}) collective-permute-start(bf16[256,128]{1,0:T(8,128)(2,1)S(1)} %get-tuple-element.33), channel_id=1, source_target_pairs={{0,2},{1,3},{2,0},{3,1},{4,6},{5,7},{6,4},{7,5},{8,10},{9,11},{10,... | collective-permute-start | bytes 196616 | tf_op jit(solution)/shard_map/ppermute | solution.py:269
  7.9 1.3 %collective-permute-start.12 = (bf16[256,128]{1,0:T(8,128)(2,1)S(1)}, bf16[256,128]{1,0:T(8,128)(2,1)S(1)}, u32[]{:S(2)}, u32[]{:S(2)}) collective-permute-start(bf16[256,128]{1,0:T(8,128)(2,1)S(1)} %get-tuple-element.34), channel_id=1, source_target_pairs={{0,3},{1,0},{2,1},{3,2},{4,7},{5,4},{6,5},{7,6},{8,11},{9,8},{10,9... | collective-permute-start | bytes 196616 | tf_op jit(solution)/shard_map/ppermute | solution.py:269
  9.3 0.1 shard_map.47
  9.4 0.7 collective-permute-start.3
  10.1 0.3 collective-permute-start.4
  10.6 2.9 %collective-permute-start.5 = (bf16[256,128]{1,0:T(8,128)(2,1)S(1)}, bf16[256,128]{1,0:T(8,128)(2,1)S(1)}, u32[]{:S(2)}, u32[]{:S(2)}) collective-permute-start(bf16[256,128]{1,0:T(8,128)(2,1)S(1)} %get-tuple-element.30), channel_id=1, source_target_pairs={{0,3},{1,0},{2,1},{3,2},{4,7},{5,4},{6,5},{7,6},{8,11},{9,8},{10,9... | collective-permute-start | bytes 196616 | tf_op jit(solution)/shard_map/ppermute | solution.py:269
  13.5 0.0 collective-permute-done.12
  13.5 3.4 %collective-permute-start.13 = (bf16[1024,128]{1,0:T(8,128)(2,1)S(1)}, bf16[1024,128]{1,0:T(8,128)(2,1)S(1)}, u32[]{:S(2)}, u32[]{:S(2)}) collective-permute-start(bf16[1024,128]{1,0:T(8,128)(2,1)S(1)} %constant_dynamic-update-slice_fusion.refs_1_), channel_id=1, source_target_pairs={{0,16},{4,20},{8,24},{12,28},{1,17},{5,21},{9,25},{13,29},{2,18},{... | collective-permute-start | bytes 786440 | tf_op jit(solution)/shard_map/ppermute | solution.py:280
  17.0 0.0 collective-permute-done.3
  17.0 1.0 %collective-permute-done.4 = bf16[256,128]{1,0:T(8,128)(2,1)S(1)} collective-permute-done((bf16[256,128]{1,0:T(8,128)(2,1)S(1)}, bf16[256,128]{1,0:T(8,128)(2,1)S(1)}, u32[]{:S(2)}, u32[]{:S(2)}) %collective-permute-start.4) | collective-permute-done | bytes 65568 | tf_op jit(solution)/shard_map/ppermute | solution.py:269
  18.0 0.0 collective-permute-done.5
  18.1 3.7 %collective-permute-start.6 = (bf16[1024,128]{1,0:T(8,128)(2,1)S(1)}, bf16[1024,128]{1,0:T(8,128)(2,1)S(1)}, u32[]{:S(2)}, u32[]{:S(2)}) collective-permute-start(bf16[1024,128]{1,0:T(8,128)(2,1)S(1)} %constant_dynamic-update-slice_fusion.4.refs_0_), channel_id=1, source_target_pairs={{0,16},{4,20},{8,24},{12,28},{1,17},{5,21},{9,25},{13,29},{2,18},{... | collective-permute-start | bytes 786440 | tf_op jit(solution)/shard_map/ppermute | solution.py:280
  21.7 1.6 %collective-permute-start = (bf16[256,256]{1,0:T(8,128)(2,1)S(1)}, bf16[256,256]{1,0:T(8,128)(2,1)S(1)}, u32[]{:S(2)}, u32[]{:S(2)}) collective-permute-start(bf16[256,256]{1,0:T(8,128)(2,1)S(1)} %get-tuple-element.24), channel_id=1, source_target_pairs={{0,1},{1,2},{2,3},{3,0},{4,5},{5,6},{6,7},{7,4},{8,9},{9,10},{10,1... | collective-permute-start | bytes 393224 | tf_op jit(solution)/shard_map/ppermute | solution.py:269
  23.3 2.0 %collective-permute-start.1 = (bf16[256,256]{1,0:T(8,128)(2,1)S(1)}, bf16[256,256]{1,0:T(8,128)(2,1)S(1)}, u32[]{:S(2)}, u32[]{:S(2)}) collective-permute-start(bf16[256,256]{1,0:T(8,128)(2,1)S(1)} %get-tuple-element.25), channel_id=1, source_target_pairs={{0,2},{1,3},{2,0},{3,1},{4,6},{5,7},{6,4},{7,5},{8,10},{9,11},{10,... | collective-permute-start | bytes 393224 | tf_op jit(solution)/shard_map/ppermute | solution.py:269
  25.4 3.4 %collective-permute-start.15 = (bf16[1024,128]{1,0:T(8,128)(2,1)S(1)}, bf16[1024,128]{1,0:T(8,128)(2,1)S(1)}, u32[]{:S(2)}, u32[]{:S(2)}) collective-permute-start(bf16[1024,128]{1,0:T(8,128)(2,1)S(1)} %constant_dynamic-update-slice_fusion.refs_1_), channel_id=1, source_target_pairs={{0,8},{4,12},{8,16},{16,24},{20,28},{1,9},{5,13},{9,17},{17,25},{2... | collective-permute-start | bytes 786440 | tf_op jit(solution)/shard_map/ppermute | solution.py:280
  28.8 0.0 collective-permute-done.13.refs_1_
  28.8 0.7 collective-permute-start.14
  29.6 0.8 %collective-permute-start.2 = (bf16[256,256]{1,0:T(8,128)(2,1)S(1)}, bf16[256,256]{1,0:T(8,128)(2,1)S(1)}, u32[]{:S(2)}, u32[]{:S(2)}) collective-permute-start(bf16[256,256]{1,0:T(8,128)(2,1)S(1)} %get-tuple-element.26), channel_id=1, source_target_pairs={{0,3},{1,0},{2,1},{3,2},{4,7},{5,4},{6,5},{7,6},{8,11},{9,8},{10,9... | collective-permute-start | bytes 393224 | tf_op jit(solution)/shard_map/ppermute | solution.py:269
  30.5 3.4 %collective-permute-done.1 = bf16[256,256]{1,0:T(8,128)(2,1)S(1)} collective-permute-done((bf16[256,256]{1,0:T(8,128)(2,1)S(1)}, bf16[256,256]{1,0:T(8,128)(2,1)S(1)}, u32[]{:S(2)}, u32[]{:S(2)}) %collective-permute-start.1) | collective-permute-done | bytes 131104 | tf_op jit(solution)/shard_map/ppermute | solution.py:269
  33.8 3.4 %collective-permute-start.8 = (bf16[1024,128]{1,0:T(8,128)(2,1)S(1)}, bf16[1024,128]{1,0:T(8,128)(2,1)S(1)}, u32[]{:S(2)}, u32[]{:S(2)}) collective-permute-start(bf16[1024,128]{1,0:T(8,128)(2,1)S(1)} %constant_dynamic-update-slice_fusion.4.refs_0_), channel_id=1, source_target_pairs={{0,8},{4,12},{8,16},{16,24},{20,28},{1,9},{5,13},{9,17},{17,25},{2... | collective-permute-start | bytes 786440 | tf_op jit(solution)/shard_map/ppermute | solution.py:280
  37.2 0.7 collective-permute-start.7
  37.9 0.0 collective-permute-done.14
  38.0 0.1 collective-permute-start.16
  38.1 4.7 %collective-permute-done.8 = bf16[1024,128]{1,0:T(8,128)(2,1)S(1)} collective-permute-done((bf16[1024,128]{1,0:T(8,128)(2,1)S(1)}, bf16[1024,128]{1,0:T(8,128)(2,1)S(1)}, u32[]{:S(2)}, u32[]{:S(2)}) %collective-permute-start.8) | collective-permute-done | bytes 262176 | tf_op jit(solution)/shard_map/ppermute | solution.py:280
  42.8 0.0 collective-permute-done.7
  42.8 0.1 broadcast_select_fusion.1
  42.9 0.0 copy-start.3
  42.9 0.1 collective-permute-start.9
  43.0 0.0 collective-permute-done.2
  43.0 0.5 copy-done.3
  43.5 2.6 %shard_map.48 = (f32[2,1024,128]{2,1,0:T(8,128)S(1)}, f32[2,1024,128]{2,1,0:T(8,128)S(1)}, f32[2,1024,128]{2,1,0:T(8,128)S(1)}) custom-call(s32[1,4]{1,0:T(1,128)S(1)} %copy-done.3, bf16[1024,256]{1,0:T(8,128)(2,1)S(1)} %constant_dynamic-update-slice_fusion.8.q_ref, bf16[1024,128]{1,0:T(8,128)(2,1)S(1)} %constant_dynamic-update-slice_fusion.4.refs_0_, ...), custom_call_target="tpu_custom_call" | custom-call | flops 1073741824 | bytes 1048576 | tf_op jit(solution)/shard_map/pallas_call | solution.py:186
  46.2 4.3 %shard_map.49 = (f32[2,1024,128]{2,1,0:T(8,128)S(1)}, f32[2,1024,128]{2,1,0:T(8,128)S(1)}, f32[2,1024,128]{2,1,0:T(8,128)S(1)}) custom-call(s32[1,4]{1,0:T(1,128)S(1)} %copy-done.3, bf16[1024,256]{1,0:T(8,128)(2,1)S(1)} %constant_dynamic-update-slice_fusion.8.q_ref, ...), custom_call_target="tpu_custom_call", output_to_operand_aliasing={{0}: (4, {}), {1}: (5, {}), {2}: (6, {})} | custom-call | flops 1073741824 | bytes 1048576 | tf_op jit(solution)/shard_map/pallas_call | solution.py:186
  50.5 2.6 %shard_map.52 = bf16[2,256,128]{2,1,0:T(8,128)(2,1)S(1)} custom-call(s32[1,4]{1,0:T(1,128)S(1)} %copy-done.3, bf16[1024,256]{1,0:T(8,128)(2,1)S(1)} %constant_dynamic-update-slice_fusion.8.q_ref, bf16[1024,128]{1,0:T(8,128)(2,1)S(1)} %get-tuple-element.44.refs_0_, bf16[1024,128]{1,0:T(8,128)(2,1)S(1)} %collective-permute-done.9.refs_1_, ...), custom_call_target="tpu_custom_call" | custom-call | flops 1073741824 | bytes 2097152 | tf_op jit(solution)/shard_map/pallas_call | solution.py:186
  53.1 0.1 collective-permute-start.20
  53.1 2.6 %collective-permute-start.21 = (bf16[256,128]{1,0:T(8,128)(2,1)S(1)}, bf16[256,128]{1,0:T(8,128)(2,1)S(1)}, u32[]{:S(2)}, u32[]{:S(2)}) collective-permute-start(bf16[256,128]{1,0:T(8,128)(2,1)S(1)} %get-tuple-element.51), channel_id=1, source_target_pairs={{0,2},{1,3},{2,0},{3,1},{4,6},{5,7},{6,4},{7,5},{8,10},{9,11},{10,... | collective-permute-start | bytes 196616 | tf_op jit(solution)/shard_map/ppermute | solution.py:269
  55.7 2.6 %shard_map.51 = bf16[2,256,128]{2,1,0:T(8,128)(2,1)S(1)} custom-call(s32[1,4]{1,0:T(1,128)S(1)} %copy-done.3, bf16[1024,256]{1,0:T(8,128)(2,1)S(1)} %constant_dynamic-update-slice_fusion.8.q_ref, bf16[1024,128]{1,0:T(8,128)(2,1)S(1)} %get-tuple-element.44.refs_0_, bf16[1024,128]{1,0:T(8,128)(2,1)S(1)} %collective-permute-done.9.refs_1_, ...), custom_call_target="tpu_custom_call" | custom-call | flops 1073741824 | bytes 2097152 | tf_op jit(solution)/shard_map/pallas_call | solution.py:186
  58.3 1.5 %collective-permute-start.22 = (bf16[256,128]{1,0:T(8,128)(2,1)S(1)}, bf16[256,128]{1,0:T(8,128)(2,1)S(1)}, u32[]{:S(2)}, u32[]{:S(2)}) collective-permute-start(bf16[256,128]{1,0:T(8,128)(2,1)S(1)} %get-tuple-element.49), channel_id=1, source_target_pairs={{0,3},{1,0},{2,1},{3,2},{4,7},{5,4},{6,5},{7,6},{8,11},{9,8},{10,9... | collective-permute-start | bytes 196616 | tf_op jit(solution)/shard_map/ppermute | solution.py:269
  59.7 4.6 %shard_map.50 = bf16[4,256,128]{2,1,0:T(8,128)(2,1)S(1)} custom-call(s32[1,4]{1,0:T(1,128)S(1)} %copy-done.3, bf16[1024,256]{1,0:T(8,128)(2,1)S(1)} %constant_dynamic-update-slice_fusion.8.q_ref, bf16[1024,128]{1,0:T(8,128)(2,1)S(1)} %get-tuple-element.44.refs_0_, bf16[1024,128]{1,0:T(8,128)(2,1)S(1)} %collective-permute-done.9.refs_1_, ...), custom_call_target="tpu_custom_call" | custom-call | flops 1073741824 | bytes 2097152 | tf_op jit(solution)/shard_map/pallas_call | solution.py:186
  64.4 0.8 %collective-permute-start.17 = (bf16[256,128]{1,0:T(8,128)(2,1)S(1)}, bf16[256,128]{1,0:T(8,128)(2,1)S(1)}, u32[]{:S(2)}, u32[]{:S(2)}) collective-permute-start(bf16[256,128]{1,0:T(8,128)(2,1)S(1)} %get-tuple-element.47), channel_id=1, source_target_pairs={{0,1},{1,2},{2,3},{3,0},{4,5},{5,6},{6,7},{7,4},{8,9},{9,10},{10,1... | collective-permute-start | bytes 196616 | tf_op jit(solution)/shard_map/ppermute | solution.py:269
  65.2 1.3 %collective-permute-start.18 = (bf16[256,128]{1,0:T(8,128)(2,1)S(1)}, bf16[256,128]{1,0:T(8,128)(2,1)S(1)}, u32[]{:S(2)}, u32[]{:S(2)}) collective-permute-start(bf16[256,128]{1,0:T(8,128)(2,1)S(1)} %get-tuple-element.46), channel_id=1, source_target_pairs={{0,2},{1,3},{2,0},{3,1},{4,6},{5,7},{6,4},{7,5},{8,10},{9,11},{10,... | collective-permute-start | bytes 196616 | tf_op jit(solution)/shard_map/ppermute | solution.py:269
  66.5 2.8 %collective-permute-start.19 = (bf16[256,128]{1,0:T(8,128)(2,1)S(1)}, bf16[256,128]{1,0:T(8,128)(2,1)S(1)}, u32[]{:S(2)}, u32[]{:S(2)}) collective-permute-start(bf16[256,128]{1,0:T(8,128)(2,1)S(1)} %get-tuple-element.45), channel_id=1, source_target_pairs={{0,3},{1,0},{2,1},{3,2},{4,7},{5,4},{6,5},{7,6},{8,11},{9,8},{10,9... | collective-permute-start | bytes 196616 | tf_op jit(solution)/shard_map/ppermute | solution.py:269
  69.4 1.7 %collective-permute-done.17.refs_1_ = bf16[256,128]{1,0:T(8,128)(2,1)S(1)} collective-permute-done((bf16[256,128]{1,0:T(8,128)(2,1)S(1)}, bf16[256,128]{1,0:T(8,128)(2,1)S(1)}, u32[]{:S(2)}, u32[]{:S(2)}) %collective-permute-start.17) | collective-permute-done | bytes 65568 | tf_op jit(solution)/shard_map/ppermute | solution.py:269
  71.1 1.5 %collective-permute-done.18.refs_2_ = bf16[256,128]{1,0:T(8,128)(2,1)S(1)} collective-permute-done((bf16[256,128]{1,0:T(8,128)(2,1)S(1)}, bf16[256,128]{1,0:T(8,128)(2,1)S(1)}, u32[]{:S(2)}, u32[]{:S(2)}) %collective-permute-start.18) | collective-permute-done | bytes 65568 | tf_op jit(solution)/shard_map/ppermute | solution.py:269
  72.5 0.9 %shard_map.53 = bf16[256,1024]{1,0:T(8,128)(2,1)} custom-call(bf16[256,128]{1,0:T(8,128)(2,1)S(1)} %get-tuple-element.48.refs_0_, bf16[256,128]{1,0:T(8,128)(2,1)S(1)} %collective-permute-done.17.refs_1_, bf16[256,128]{1,0:T(8,128)(2,1)S(1)} %collective-permute-done.18.refs_2_, bf16[256,128]{1,0:T(8,128)(2,1)S(1)} %collective-permute-done.19.refs_3_, ...), custom_call_target="tpu_custom_call" | custom-call | tf_op jit(solution)/shard_map/pallas_call | solution.py:251
  (34 shorter events, 0.4 us)
Async XLA Ops:
  0.0 1.0 %copy-start = (bf16[256,1024]{1,0:T(8,128)(2,1)S(1)}, bf16[256,1024]{1,0:T(8,128)(2,1)}, u32[]{:S(2)}) copy-start(bf16[256,1024]{1,0:T(8,128)(2,1)} %refs_1_.1) | copy-start | bytes 1572868
  1.0 0.9 %copy-start.1 = (bf16[256,512]{1,0:T(8,128)(2,1)S(1)}, bf16[256,512]{1,0:T(8,128)(2,1)}, u32[]{:S(2)}) copy-start(bf16[256,512]{1,0:T(8,128)(2,1)} %refs_0_.2) | copy-start | bytes 786436
  2.0 7.3 %copy-start.2 = (bf16[256,512]{1,0:T(8,128)(2,1)S(1)}, bf16[256,512]{1,0:T(8,128)(2,1)}, u32[]{:S(2)}) copy-start(bf16[256,512]{1,0:T(8,128)(2,1)} %refs_0_.3) | copy-start | bytes 786436
  2.2 8.3 %collective-permute-start.10 = (bf16[256,128]{1,0:T(8,128)(2,1)S(1)}, bf16[256,128]{1,0:T(8,128)(2,1)S(1)}, u32[]{:S(2)}, u32[]{:S(2)}) collective-permute-start(bf16[256,128]{1,0:T(8,128)(2,1)S(1)} %get-tuple-element.32), channel_id=1, source_target_pairs={{0,1},{1,2},{2,3},{3,0},{4,5},{5,6},{6,7},{7,4},{8,9},{9,10},{10,1... | collective-permute-start | bytes 196616 | tf_op jit(solution)/shard_map/ppermute | solution.py:269
  5.3 8.1 %collective-permute-start.11 = (bf16[256,128]{1,0:T(8,128)(2,1)S(1)}, bf16[256,128]{1,0:T(8,128)(2,1)S(1)}, u32[]{:S(2)}, u32[]{:S(2)}) collective-permute-start(bf16[256,128]{1,0:T(8,128)(2,1)S(1)} %get-tuple-element.33), channel_id=1, source_target_pairs={{0,2},{1,3},{2,0},{3,1},{4,6},{5,7},{6,4},{7,5},{8,10},{9,11},{10,... | collective-permute-start | bytes 196616 | tf_op jit(solution)/shard_map/ppermute | solution.py:269
  7.9 5.6 %collective-permute-start.12 = (bf16[256,128]{1,0:T(8,128)(2,1)S(1)}, bf16[256,128]{1,0:T(8,128)(2,1)S(1)}, u32[]{:S(2)}, u32[]{:S(2)}) collective-permute-start(bf16[256,128]{1,0:T(8,128)(2,1)S(1)} %get-tuple-element.34), channel_id=1, source_target_pairs={{0,3},{1,0},{2,1},{3,2},{4,7},{5,4},{6,5},{7,6},{8,11},{9,8},{10,9... | collective-permute-start | bytes 196616 | tf_op jit(solution)/shard_map/ppermute | solution.py:269
  9.4 7.6 %collective-permute-start.3 = (bf16[256,128]{1,0:T(8,128)(2,1)S(1)}, bf16[256,128]{1,0:T(8,128)(2,1)S(1)}, u32[]{:S(2)}, u32[]{:S(2)}) collective-permute-start(bf16[256,128]{1,0:T(8,128)(2,1)S(1)} %get-tuple-element.28), channel_id=1, source_target_pairs={{0,1},{1,2},{2,3},{3,0},{4,5},{5,6},{6,7},{7,4},{8,9},{9,10},{10,1... | collective-permute-start | bytes 196616 | tf_op jit(solution)/shard_map/ppermute | solution.py:269
  10.1 7.9 %collective-permute-start.4 = (bf16[256,128]{1,0:T(8,128)(2,1)S(1)}, bf16[256,128]{1,0:T(8,128)(2,1)S(1)}, u32[]{:S(2)}, u32[]{:S(2)}) collective-permute-start(bf16[256,128]{1,0:T(8,128)(2,1)S(1)} %get-tuple-element.29), channel_id=1, source_target_pairs={{0,2},{1,3},{2,0},{3,1},{4,6},{5,7},{6,4},{7,5},{8,10},{9,11},{10,... | collective-permute-start | bytes 196616 | tf_op jit(solution)/shard_map/ppermute | solution.py:269
  10.6 7.5 %collective-permute-start.5 = (bf16[256,128]{1,0:T(8,128)(2,1)S(1)}, bf16[256,128]{1,0:T(8,128)(2,1)S(1)}, u32[]{:S(2)}, u32[]{:S(2)}) collective-permute-start(bf16[256,128]{1,0:T(8,128)(2,1)S(1)} %get-tuple-element.30), channel_id=1, source_target_pairs={{0,3},{1,0},{2,1},{3,2},{4,7},{5,4},{6,5},{7,6},{8,11},{9,8},{10,9... | collective-permute-start | bytes 196616 | tf_op jit(solution)/shard_map/ppermute | solution.py:269
  13.5 15.3 %collective-permute-start.13 = (bf16[1024,128]{1,0:T(8,128)(2,1)S(1)}, bf16[1024,128]{1,0:T(8,128)(2,1)S(1)}, u32[]{:S(2)}, u32[]{:S(2)}) collective-permute-start(bf16[1024,128]{1,0:T(8,128)(2,1)S(1)} %constant_dynamic-update-slice_fusion.refs_1_), channel_id=1, source_target_pairs={{0,16},{4,20},{8,24},{12,28},{1,17},{5,21},{9,25},{13,29},{2,18},{... | collective-permute-start | bytes 786440 | tf_op jit(solution)/shard_map/ppermute | solution.py:280
  18.1 19.1 %collective-permute-start.6 = (bf16[1024,128]{1,0:T(8,128)(2,1)S(1)}, bf16[1024,128]{1,0:T(8,128)(2,1)S(1)}, u32[]{:S(2)}, u32[]{:S(2)}) collective-permute-start(bf16[1024,128]{1,0:T(8,128)(2,1)S(1)} %constant_dynamic-update-slice_fusion.4.refs_0_), channel_id=1, source_target_pairs={{0,16},{4,20},{8,24},{12,28},{1,17},{5,21},{9,25},{13,29},{2,18},{... | collective-permute-start | bytes 786440 | tf_op jit(solution)/shard_map/ppermute | solution.py:280
  21.7 7.9 %collective-permute-start = (bf16[256,256]{1,0:T(8,128)(2,1)S(1)}, bf16[256,256]{1,0:T(8,128)(2,1)S(1)}, u32[]{:S(2)}, u32[]{:S(2)}) collective-permute-start(bf16[256,256]{1,0:T(8,128)(2,1)S(1)} %get-tuple-element.24), channel_id=1, source_target_pairs={{0,1},{1,2},{2,3},{3,0},{4,5},{5,6},{6,7},{7,4},{8,9},{9,10},{10,1... | collective-permute-start | bytes 393224 | tf_op jit(solution)/shard_map/ppermute | solution.py:269
  23.3 10.5 %collective-permute-start.1 = (bf16[256,256]{1,0:T(8,128)(2,1)S(1)}, bf16[256,256]{1,0:T(8,128)(2,1)S(1)}, u32[]{:S(2)}, u32[]{:S(2)}) collective-permute-start(bf16[256,256]{1,0:T(8,128)(2,1)S(1)} %get-tuple-element.25), channel_id=1, source_target_pairs={{0,2},{1,3},{2,0},{3,1},{4,6},{5,7},{6,4},{7,5},{8,10},{9,11},{10,... | collective-permute-start | bytes 393224 | tf_op jit(solution)/shard_map/ppermute | solution.py:269
  25.4 12.5 %collective-permute-start.15 = (bf16[1024,128]{1,0:T(8,128)(2,1)S(1)}, bf16[1024,128]{1,0:T(8,128)(2,1)S(1)}, u32[]{:S(2)}, u32[]{:S(2)}) collective-permute-start(bf16[1024,128]{1,0:T(8,128)(2,1)S(1)} %constant_dynamic-update-slice_fusion.refs_1_), channel_id=1, source_target_pairs={{0,8},{4,12},{8,16},{16,24},{20,28},{1,9},{5,13},{9,17},{17,25},{2... | collective-permute-start | bytes 786440 | tf_op jit(solution)/shard_map/ppermute | solution.py:280
  28.8 9.1 %collective-permute-start.14 = (bf16[1024,128]{1,0:T(8,128)(2,1)S(1)}, bf16[1024,128]{1,0:T(8,128)(2,1)S(1)}, u32[]{:S(2)}, u32[]{:S(2)}) collective-permute-start(bf16[1024,128]{1,0:T(8,128)(2,1)S(1)} %collective-permute-done.13.refs_1_), channel_id=1, source_target_pairs={{28,20},{29,21},{30,22},{31,23}} | collective-permute-start | bytes 786440 | tf_op jit(solution)/shard_map/ppermute | solution.py:280
  29.6 13.4 %collective-permute-start.2 = (bf16[256,256]{1,0:T(8,128)(2,1)S(1)}, bf16[256,256]{1,0:T(8,128)(2,1)S(1)}, u32[]{:S(2)}, u32[]{:S(2)}) collective-permute-start(bf16[256,256]{1,0:T(8,128)(2,1)S(1)} %get-tuple-element.26), channel_id=1, source_target_pairs={{0,3},{1,0},{2,1},{3,2},{4,7},{5,4},{6,5},{7,6},{8,11},{9,8},{10,9... | collective-permute-start | bytes 393224 | tf_op jit(solution)/shard_map/ppermute | solution.py:269
  33.8 9.0 %collective-permute-start.8 = (bf16[1024,128]{1,0:T(8,128)(2,1)S(1)}, bf16[1024,128]{1,0:T(8,128)(2,1)S(1)}, u32[]{:S(2)}, u32[]{:S(2)}) collective-permute-start(bf16[1024,128]{1,0:T(8,128)(2,1)S(1)} %constant_dynamic-update-slice_fusion.4.refs_0_), channel_id=1, source_target_pairs={{0,8},{4,12},{8,16},{16,24},{20,28},{1,9},{5,13},{9,17},{17,25},{2... | collective-permute-start | bytes 786440 | tf_op jit(solution)/shard_map/ppermute | solution.py:280
  37.2 5.6 %collective-permute-start.7 = (bf16[1024,128]{1,0:T(8,128)(2,1)S(1)}, bf16[1024,128]{1,0:T(8,128)(2,1)S(1)}, u32[]{:S(2)}, u32[]{:S(2)}) collective-permute-start(bf16[1024,128]{1,0:T(8,128)(2,1)S(1)} %collective-permute-done.6.refs_0_), channel_id=1, source_target_pairs={{28,20},{29,21},{30,22},{31,23}} | collective-permute-start | bytes 786440 | tf_op jit(solution)/shard_map/ppermute | solution.py:280
  38.0 12.5 %collective-permute-start.16 = (bf16[1024,128]{1,0:T(8,128)(2,1)S(1)}, bf16[1024,128]{1,0:T(8,128)(2,1)S(1)}, u32[]{:S(2)}, u32[]{:S(2)}) collective-permute-start(bf16[1024,128]{1,0:T(8,128)(2,1)S(1)} %get-tuple-element.41), channel_id=1, source_target_pairs={{0,4},{4,0},{8,12},{12,8},{16,20},{20,16},{24,28},{28,24},{1,5},{5... | collective-permute-start | bytes 786440 | tf_op jit(solution)/shard_map/ppermute | solution.py:280
  42.9 0.7 copy-start.3
  42.9 7.6 %collective-permute-start.9 = (bf16[1024,128]{1,0:T(8,128)(2,1)S(1)}, bf16[1024,128]{1,0:T(8,128)(2,1)S(1)}, u32[]{:S(2)}, u32[]{:S(2)}) collective-permute-start(bf16[1024,128]{1,0:T(8,128)(2,1)S(1)} %get-tuple-element.43), channel_id=1, source_target_pairs={{0,4},{4,0},{8,12},{12,8},{16,20},{20,16},{24,28},{28,24},{1,5},{5... | collective-permute-start | bytes 786440 | tf_op jit(solution)/shard_map/ppermute | solution.py:280
  53.1 13.5 %collective-permute-start.20 = (bf16[256,128]{1,0:T(8,128)(2,1)S(1)}, bf16[256,128]{1,0:T(8,128)(2,1)S(1)}, u32[]{:S(2)}, u32[]{:S(2)}) collective-permute-start(bf16[256,128]{1,0:T(8,128)(2,1)S(1)} %get-tuple-element.52), channel_id=1, source_target_pairs={{0,1},{1,2},{2,3},{3,0},{4,5},{5,6},{6,7},{7,4},{8,9},{9,10},{10,1... | collective-permute-start | bytes 196616 | tf_op jit(solution)/shard_map/ppermute | solution.py:269
  53.1 16.2 %collective-permute-start.21 = (bf16[256,128]{1,0:T(8,128)(2,1)S(1)}, bf16[256,128]{1,0:T(8,128)(2,1)S(1)}, u32[]{:S(2)}, u32[]{:S(2)}) collective-permute-start(bf16[256,128]{1,0:T(8,128)(2,1)S(1)} %get-tuple-element.51), channel_id=1, source_target_pairs={{0,2},{1,3},{2,0},{3,1},{4,6},{5,7},{6,4},{7,5},{8,10},{9,11},{10,... | collective-permute-start | bytes 196616 | tf_op jit(solution)/shard_map/ppermute | solution.py:269
  58.3 11.1 %collective-permute-start.22 = (bf16[256,128]{1,0:T(8,128)(2,1)S(1)}, bf16[256,128]{1,0:T(8,128)(2,1)S(1)}, u32[]{:S(2)}, u32[]{:S(2)}) collective-permute-start(bf16[256,128]{1,0:T(8,128)(2,1)S(1)} %get-tuple-element.49), channel_id=1, source_target_pairs={{0,3},{1,0},{2,1},{3,2},{4,7},{5,4},{6,5},{7,6},{8,11},{9,8},{10,9... | collective-permute-start | bytes 196616 | tf_op jit(solution)/shard_map/ppermute | solution.py:269
  64.4 6.7 %collective-permute-start.17 = (bf16[256,128]{1,0:T(8,128)(2,1)S(1)}, bf16[256,128]{1,0:T(8,128)(2,1)S(1)}, u32[]{:S(2)}, u32[]{:S(2)}) collective-permute-start(bf16[256,128]{1,0:T(8,128)(2,1)S(1)} %get-tuple-element.47), channel_id=1, source_target_pairs={{0,1},{1,2},{2,3},{3,0},{4,5},{5,6},{6,7},{7,4},{8,9},{9,10},{10,1... | collective-permute-start | bytes 196616 | tf_op jit(solution)/shard_map/ppermute | solution.py:269
  65.2 7.3 %collective-permute-start.18 = (bf16[256,128]{1,0:T(8,128)(2,1)S(1)}, bf16[256,128]{1,0:T(8,128)(2,1)S(1)}, u32[]{:S(2)}, u32[]{:S(2)}) collective-permute-start(bf16[256,128]{1,0:T(8,128)(2,1)S(1)} %get-tuple-element.46), channel_id=1, source_target_pairs={{0,2},{1,3},{2,0},{3,1},{4,6},{5,7},{6,4},{7,5},{8,10},{9,11},{10,... | collective-permute-start | bytes 196616 | tf_op jit(solution)/shard_map/ppermute | solution.py:269
  66.5 6.0 %collective-permute-start.19 = (bf16[256,128]{1,0:T(8,128)(2,1)S(1)}, bf16[256,128]{1,0:T(8,128)(2,1)S(1)}, u32[]{:S(2)}, u32[]{:S(2)}) collective-permute-start(bf16[256,128]{1,0:T(8,128)(2,1)S(1)} %get-tuple-element.45), channel_id=1, source_target_pairs={{0,3},{1,0},{2,1},{3,2},{4,7},{5,4},{6,5},{7,6},{8,11},{9,8},{10,9... | collective-permute-start | bytes 196616 | tf_op jit(solution)/shard_map/ppermute | solution.py:269

commit v3 on v2

--- a/solution.py
+++ b/solution.py
@@ -59,17 +59,18 @@
         else:
             offsets = list(range(0, tokens, tile))
 
-        def finish(number, base, numer, total):
+        def finish(member, number, base, numer, total):
+            columns = pl.ds(members.index(member) * HEAD_SIZE, HEAD_SIZE)
             out = (numer / jnp.sum(total, axis=1, keepdims=True)).astype(o_ref.dtype)
             if by_goal:
                 each = share // tile
-                o_ref[number // each, pl.ds(number % each * tile, tile), :] = out
+                o_ref[number // each, pl.ds(number % each * tile, tile), columns] = out
                 return
             size = min(share, tile)
             for part in range(0, tile, size):
                 start = base + part
                 goal = lax.rem(start // share + heads - place, heads)
-                o_ref[goal, pl.ds(start % share, size), :] = out[part : part + size, :]
+                o_ref[goal, pl.ds(start % share, size), columns] = out[part : part + size, :]
 
         def run(items):
             at = lambda i: offsets[items[i][3]]
@@ -139,7 +140,7 @@
                 if not (begin and slot == 0):
                     numer = numer_run[member, rows, :] + numer
                 if last and slot == len(slots) - 1:
-                    finish(number, at(i), numer, total_run[member, rows, :])
+                    finish(member, number, at(i), numer, total_run[member, rows, :])
                 else:
                     numer_run[member, rows, :] = numer
 
@@ -175,7 +176,9 @@
     whole = jax.ShapeDtypeStruct((QUERY_PER_KV, tokens, LANES), jnp.float32)
     scratch = [pltpu.VMEM((tile, tokens), jnp.float32)] * 2 + [pltpu.VMEM((tile, tokens), jnp.bfloat16)] * 2
     if last:
-        out_shape = jax.ShapeDtypeStruct((len(goes) if by_goal else heads, share, HEAD_SIZE), queries.dtype)
+        out_shape = jax.ShapeDtypeStruct(
+            (len(goes) if by_goal else heads, share, len(members) * HEAD_SIZE), queries.dtype
+        )
         scratch += [pltpu.VMEM(whole.shape, jnp.float32)] * 3
     else:
         out_shape = [whole] * n_state
@@ -269,7 +272,9 @@
         return lax.ppermute(piece, "head", [(i, (i + by) % heads) for i in range(heads)])
 
     def gather_tokens(pieces):
-        got = [piece if j == 0 else rotate(piece, j) for j, piece in enumerate(pieces)]
+        got = {0: pieces[0]}
+        for j in sorted(range(1, heads), key=lambda j: abs(2 * j - heads)):
+            got[j] = rotate(pieces[j], j)
         whole = jnp.zeros((tokens, pieces[0].shape[1]), pieces[0].dtype)
         for j in range(heads):
             source = lax.rem(place + heads - j, heads)
@@ -315,19 +320,15 @@
     state = attend(visible, query_own, members, [(0, key_own, value_own)], None, False)
     if far:
         state = attend(visible, query_own, members, far, state, False)
-    pieces = []
-    tile = min(TILE, tokens)
-    for member in members:
-        groups = [None]
-        if member == members[-1] and share % tile == 0 and heads > 2:
-            cut = heads // 2 + 1
-            groups = [list(range(1, cut)), list(range(cut, heads)) + [0]]
-        got = {}
-        for goes in groups:
-            out = attend(visible, query_own, [member], near, state, True, goes)
-            for i, j in enumerate(goes or range(heads)):
-                got[j] = rotate(out[i], j) if j else out[i]
-        pieces.append([got[j] for j in range(heads)])
+    groups = [None]
+    if share % min(TILE, tokens) == 0:
+        groups = [[j] for j in sorted(range(1, heads), key=lambda j: abs(2 * j - heads))] + [[0]]
+    got = {}
+    for goes in groups:
+        out = attend(visible, query_own, members, near, state, True, goes)
+        for i, j in enumerate(goes or range(heads)):
+            got[j] = rotate(out[i], j) if j else out[i]
+    pieces = [[got[j] for j in range(heads)]]
     return join_heads(pieces)
 
 

time: 73.7 us -> 70.1 us (0.951)
  starting transfers between devices: 39.9 us -> 33.8 us
  waiting for transfers between devices: 12.3 us -> 14.5 us
    ppermute x15 -> x12, starting transfers between devices: 24.6 us -> 18.4 us  [rotate(): lax.ppermute(piece, 'head', [(i, (i + by) % heads) for i in range(heads)])]
    ppermute x15 -> x12, waiting for transfers between devices: 7.54 us -> 9.72 us  [rotate(): lax.ppermute(piece, 'head', [(i, (i + by) % heads) for i in range(heads)])]
    pallas_call x5 -> x6, Pallas kernels: 16.6 us -> 17.1 us  [attend(): pl.pallas_call(kernel, out_shape=out_shape, in_specs=[pl.BlockSpec(memory...]
  transfers between devices with their start and end apart: 23 -> 20, of which waited for: 5 -> 4; matrix products, arithmetic and copies ran while one was open for 1% -> 1% of each run, Pallas kernels for 19% -> 21%
where the time goes in v3:
time: 70.1 us; the launch traced here: 69.8 us
  starting transfers between devices  33.8 us (48%)
  Pallas kernels  18.3 us (26%)
  waiting for transfers between devices  14.5 us (21%)
  local copies, waits for them, and re-layouts  2.84 us (4%)
    ppermute x12, starting transfers between devices, rotate(): lax.ppermute(piece, 'head', [(i, (i + by) % heads) for i in range(heads)])  18.4 us
    pallas_call x6, Pallas kernels, attend(): pl.pallas_call(kernel, out_shape=out_shape, in_specs=[pl.BlockSpec(memory...  17.1 us
    ppermute x8, starting transfers between devices, move(): lax.ppermute(array, 'seq', [p for p in pairs if 0 <= min(p) and max(p) <...  15.3 us
    ppermute x12, waiting for transfers between devices, rotate(): lax.ppermute(piece, 'head', [(i, (i + by) % heads) for i in range(heads)])  9.72 us
    ppermute x8, waiting for transfers between devices, move(): lax.ppermute(array, 'seq', [p for p in pairs if 0 <= min(p) and max(p) <...  4.76 us
    unnamed x8, local copies, waits for them, and re-layouts  2.53 us
  transfers between devices with their start and end apart: 20, of which 4 were waited for; matrix products, arithmetic and copies ran while one was open for 1% of the time, Pallas kernels for 21%

profile of v3, /device:TPU:0, one launch (start us, length us, event | category | flops | bytes accessed | tf_op | source)
XLA Modules:
  0.0 69.8 jit_solution(13569610504532380761)
XLA Ops:
  0.0 1.0 %copy-done = bf16[256,1024]{1,0:T(8,128)(2,1)S(1)} copy-done((bf16[256,1024]{1,0:T(8,128)(2,1)S(1)}, bf16[256,1024]{1,0:T(8,128)(2,1)}, u32[]{:S(2)}) %copy-start) | copy-done | bytes 524312
  1.0 0.9 %copy-done.1 = bf16[256,512]{1,0:T(8,128)(2,1)S(1)} copy-done((bf16[256,512]{1,0:T(8,128)(2,1)S(1)}, bf16[256,512]{1,0:T(8,128)(2,1)}, u32[]{:S(2)}) %copy-start.1) | copy-done | bytes 262168
  2.0 0.2 shard_map.46
  2.2 3.1 %collective-permute-start.10 = (bf16[256,128]{1,0:T(8,128)(2,1)S(1)}, bf16[256,128]{1,0:T(8,128)(2,1)S(1)}, u32[]{:S(2)}, u32[]{:S(2)}) collective-permute-start(bf16[256,128]{1,0:T(8,128)(2,1)S(1)} %get-tuple-element.32), channel_id=1, source_target_pairs={{0,1},{1,2},{2,3},{3,0},{4,5},{5,6},{6,7},{7,4},{8,9},{9,10},{10,1... | collective-permute-start | bytes 196616 | tf_op jit(solution)/shard_map/ppermute | solution.py:272
  5.3 2.6 %collective-permute-start.11 = (bf16[256,128]{1,0:T(8,128)(2,1)S(1)}, bf16[256,128]{1,0:T(8,128)(2,1)S(1)}, u32[]{:S(2)}, u32[]{:S(2)}) collective-permute-start(bf16[256,128]{1,0:T(8,128)(2,1)S(1)} %get-tuple-element.33), channel_id=1, source_target_pairs={{0,2},{1,3},{2,0},{3,1},{4,6},{5,7},{6,4},{7,5},{8,10},{9,11},{10,... | collective-permute-start | bytes 196616 | tf_op jit(solution)/shard_map/ppermute | solution.py:272
  7.9 1.3 %collective-permute-start.12 = (bf16[256,128]{1,0:T(8,128)(2,1)S(1)}, bf16[256,128]{1,0:T(8,128)(2,1)S(1)}, u32[]{:S(2)}, u32[]{:S(2)}) collective-permute-start(bf16[256,128]{1,0:T(8,128)(2,1)S(1)} %get-tuple-element.34), channel_id=1, source_target_pairs={{0,3},{1,0},{2,1},{3,2},{4,7},{5,4},{6,5},{7,6},{8,11},{9,8},{10,9... | collective-permute-start | bytes 196616 | tf_op jit(solution)/shard_map/ppermute | solution.py:272
  9.3 0.1 shard_map.47
  9.4 0.7 %collective-permute-start.3 = (bf16[256,128]{1,0:T(8,128)(2,1)S(1)}, bf16[256,128]{1,0:T(8,128)(2,1)S(1)}, u32[]{:S(2)}, u32[]{:S(2)}) collective-permute-start(bf16[256,128]{1,0:T(8,128)(2,1)S(1)} %get-tuple-element.28), channel_id=1, source_target_pairs={{0,1},{1,2},{2,3},{3,0},{4,5},{5,6},{6,7},{7,4},{8,9},{9,10},{10,1... | collective-permute-start | bytes 196616 | tf_op jit(solution)/shard_map/ppermute | solution.py:272
  10.1 0.3 collective-permute-start.4
  10.6 0.0 collective-permute-done.10
  10.6 2.9 %collective-permute-start.5 = (bf16[256,128]{1,0:T(8,128)(2,1)S(1)}, bf16[256,128]{1,0:T(8,128)(2,1)S(1)}, u32[]{:S(2)}, u32[]{:S(2)}) collective-permute-start(bf16[256,128]{1,0:T(8,128)(2,1)S(1)} %get-tuple-element.30), channel_id=1, source_target_pairs={{0,3},{1,0},{2,1},{3,2},{4,7},{5,4},{6,5},{7,6},{8,11},{9,8},{10,9... | collective-permute-start | bytes 196616 | tf_op jit(solution)/shard_map/ppermute | solution.py:272
  13.4 0.0 collective-permute-done.11
  13.5 0.0 collective-permute-done.12
  13.5 3.4 %collective-permute-start.13 = (bf16[1024,128]{1,0:T(8,128)(2,1)S(1)}, bf16[1024,128]{1,0:T(8,128)(2,1)S(1)}, u32[]{:S(2)}, u32[]{:S(2)}) collective-permute-start(bf16[1024,128]{1,0:T(8,128)(2,1)S(1)} %constant_dynamic-update-slice_fusion.refs_1_), channel_id=1, source_target_pairs={{0,16},{4,20},{8,24},{12,28},{1,17},{5,21},{9,25},{13,29},{2,18},{... | collective-permute-start | bytes 786440 | tf_op jit(solution)/shard_map/ppermute | solution.py:285
  17.0 0.0 collective-permute-done.3
  17.0 1.0 %collective-permute-done.4 = bf16[256,128]{1,0:T(8,128)(2,1)S(1)} collective-permute-done((bf16[256,128]{1,0:T(8,128)(2,1)S(1)}, bf16[256,128]{1,0:T(8,128)(2,1)S(1)}, u32[]{:S(2)}, u32[]{:S(2)}) %collective-permute-start.4) | collective-permute-done | bytes 65568 | tf_op jit(solution)/shard_map/ppermute | solution.py:272
  18.0 0.0 collective-permute-done.5
  18.1 3.7 %collective-permute-start.6 = (bf16[1024,128]{1,0:T(8,128)(2,1)S(1)}, bf16[1024,128]{1,0:T(8,128)(2,1)S(1)}, u32[]{:S(2)}, u32[]{:S(2)}) collective-permute-start(bf16[1024,128]{1,0:T(8,128)(2,1)S(1)} %constant_dynamic-update-slice_fusion.4.refs_0_), channel_id=1, source_target_pairs={{0,16},{4,20},{8,24},{12,28},{1,17},{5,21},{9,25},{13,29},{2,18},{... | collective-permute-start | bytes 786440 | tf_op jit(solution)/shard_map/ppermute | solution.py:285
  21.7 1.6 %collective-permute-start = (bf16[256,256]{1,0:T(8,128)(2,1)S(1)}, bf16[256,256]{1,0:T(8,128)(2,1)S(1)}, u32[]{:S(2)}, u32[]{:S(2)}) collective-permute-start(bf16[256,256]{1,0:T(8,128)(2,1)S(1)} %get-tuple-element.24), channel_id=1, source_target_pairs={{0,1},{1,2},{2,3},{3,0},{4,5},{5,6},{6,7},{7,4},{8,9},{9,10},{10,1... | collective-permute-start | bytes 393224 | tf_op jit(solution)/shard_map/ppermute | solution.py:272
  23.3 2.0 %collective-permute-start.1 = (bf16[256,256]{1,0:T(8,128)(2,1)S(1)}, bf16[256,256]{1,0:T(8,128)(2,1)S(1)}, u32[]{:S(2)}, u32[]{:S(2)}) collective-permute-start(bf16[256,256]{1,0:T(8,128)(2,1)S(1)} %get-tuple-element.25), channel_id=1, source_target_pairs={{0,2},{1,3},{2,0},{3,1},{4,6},{5,7},{6,4},{7,5},{8,10},{9,11},{10,... | collective-permute-start | bytes 393224 | tf_op jit(solution)/shard_map/ppermute | solution.py:272
  25.4 3.4 %collective-permute-start.15 = (bf16[1024,128]{1,0:T(8,128)(2,1)S(1)}, bf16[1024,128]{1,0:T(8,128)(2,1)S(1)}, u32[]{:S(2)}, u32[]{:S(2)}) collective-permute-start(bf16[1024,128]{1,0:T(8,128)(2,1)S(1)} %constant_dynamic-update-slice_fusion.refs_1_), channel_id=1, source_target_pairs={{0,8},{4,12},{8,16},{16,24},{20,28},{1,9},{5,13},{9,17},{17,25},{2... | collective-permute-start | bytes 786440 | tf_op jit(solution)/shard_map/ppermute | solution.py:285
  28.8 0.0 collective-permute-done.13.refs_1_
  28.8 0.7 collective-permute-start.14
  29.6 0.8 %collective-permute-start.2 = (bf16[256,256]{1,0:T(8,128)(2,1)S(1)}, bf16[256,256]{1,0:T(8,128)(2,1)S(1)}, u32[]{:S(2)}, u32[]{:S(2)}) collective-permute-start(bf16[256,256]{1,0:T(8,128)(2,1)S(1)} %get-tuple-element.26), channel_id=1, source_target_pairs={{0,3},{1,0},{2,1},{3,2},{4,7},{5,4},{6,5},{7,6},{8,11},{9,8},{10,9... | collective-permute-start | bytes 393224 | tf_op jit(solution)/shard_map/ppermute | solution.py:272
  30.5 3.4 %collective-permute-done.1 = bf16[256,256]{1,0:T(8,128)(2,1)S(1)} collective-permute-done((bf16[256,256]{1,0:T(8,128)(2,1)S(1)}, bf16[256,256]{1,0:T(8,128)(2,1)S(1)}, u32[]{:S(2)}, u32[]{:S(2)}) %collective-permute-start.1) | collective-permute-done | bytes 131104 | tf_op jit(solution)/shard_map/ppermute | solution.py:272
  33.8 3.4 %collective-permute-start.8 = (bf16[1024,128]{1,0:T(8,128)(2,1)S(1)}, bf16[1024,128]{1,0:T(8,128)(2,1)S(1)}, u32[]{:S(2)}, u32[]{:S(2)}) collective-permute-start(bf16[1024,128]{1,0:T(8,128)(2,1)S(1)} %constant_dynamic-update-slice_fusion.4.refs_0_), channel_id=1, source_target_pairs={{0,8},{4,12},{8,16},{16,24},{20,28},{1,9},{5,13},{9,17},{17,25},{2... | collective-permute-start | bytes 786440 | tf_op jit(solution)/shard_map/ppermute | solution.py:285
  37.2 0.7 collective-permute-start.7
  37.9 0.0 collective-permute-done.14
  38.0 0.1 collective-permute-start.16
  38.1 4.7 %collective-permute-done.8 = bf16[1024,128]{1,0:T(8,128)(2,1)S(1)} collective-permute-done((bf16[1024,128]{1,0:T(8,128)(2,1)S(1)}, bf16[1024,128]{1,0:T(8,128)(2,1)S(1)}, u32[]{:S(2)}, u32[]{:S(2)}) %collective-permute-start.8) | collective-permute-done | bytes 262176 | tf_op jit(solution)/shard_map/ppermute | solution.py:285
  42.8 0.0 collective-permute-done.7
  42.9 0.0 copy-start.3
  42.9 0.1 collective-permute-start.9
  43.0 0.5 copy-done.3
  43.5 2.6 %shard_map.48 = (f32[2,1024,128]{2,1,0:T(8,128)S(1)}, f32[2,1024,128]{2,1,0:T(8,128)S(1)}, f32[2,1024,128]{2,1,0:T(8,128)S(1)}) custom-call(s32[1,4]{1,0:T(1,128)S(1)} %copy-done.3, bf16[1024,256]{1,0:T(8,128)(2,1)S(1)} %constant_dynamic-update-slice_fusion.8.q_ref, bf16[1024,128]{1,0:T(8,128)(2,1)S(1)} %constant_dynamic-update-slice_fusion.4.refs_0_, ...), custom_call_target="tpu_custom_call" | custom-call | flops 1073741824 | bytes 1048576 | tf_op jit(solution)/shard_map/pallas_call | solution.py:189
  46.2 4.3 %shard_map.49 = (f32[2,1024,128]{2,1,0:T(8,128)S(1)}, f32[2,1024,128]{2,1,0:T(8,128)S(1)}, f32[2,1024,128]{2,1,0:T(8,128)S(1)}) custom-call(s32[1,4]{1,0:T(1,128)S(1)} %copy-done.3, bf16[1024,256]{1,0:T(8,128)(2,1)S(1)} %constant_dynamic-update-slice_fusion.8.q_ref, ...), custom_call_target="tpu_custom_call", output_to_operand_aliasing={{0}: (4, {}), {1}: (5, {}), {2}: (6, {})} | custom-call | flops 1073741824 | bytes 1048576 | tf_op jit(solution)/shard_map/pallas_call | solution.py:189
  50.5 0.0 collective-permute-done.16.refs_3_
  50.5 2.5 %shard_map.53 = bf16[1,256,256]{2,1,0:T(8,128)(2,1)S(1)} custom-call(s32[1,4]{1,0:T(1,128)S(1)} %copy-done.3, bf16[1024,256]{1,0:T(8,128)(2,1)S(1)} %constant_dynamic-update-slice_fusion.8.q_ref, bf16[1024,128]{1,0:T(8,128)(2,1)S(1)} %get-tuple-element.44.refs_0_, bf16[1024,128]{1,0:T(8,128)(2,1)S(1)} %collective-permute-done.9.refs_1_, ...), custom_call_target="tpu_custom_call" | custom-call | flops 2147483648 | bytes 2097152 | tf_op jit(solution)/shard_map/pallas_call | solution.py:189
  53.0 2.2 %collective-permute-start.19 = (bf16[256,256]{1,0:T(8,128)(2,1)S(1)}, bf16[256,256]{1,0:T(8,128)(2,1)S(1)}, u32[]{:S(2)}, u32[]{:S(2)}) collective-permute-start(bf16[256,256]{1,0:T(8,128)(2,1)S(1)} %bitcast.5), channel_id=1, source_target_pairs={{0,3},{1,0},{2,1},{3,2},{4,7},{5,4},{6,5},{7,6},{8,11},{9,8},{10,9... | collective-permute-start | bytes 393224 | tf_op jit(solution)/shard_map/ppermute | solution.py:272
  55.3 2.5 %shard_map.52 = bf16[1,256,256]{2,1,0:T(8,128)(2,1)S(1)} custom-call(s32[1,4]{1,0:T(1,128)S(1)} %copy-done.3, bf16[1024,256]{1,0:T(8,128)(2,1)S(1)} %constant_dynamic-update-slice_fusion.8.q_ref, bf16[1024,128]{1,0:T(8,128)(2,1)S(1)} %get-tuple-element.44.refs_0_, bf16[1024,128]{1,0:T(8,128)(2,1)S(1)} %collective-permute-done.9.refs_1_, ...), custom_call_target="tpu_custom_call" | custom-call | flops 2147483648 | bytes 2097152 | tf_op jit(solution)/shard_map/pallas_call | solution.py:189
  57.8 0.1 collective-permute-start.18
  57.9 2.5 %shard_map.51 = bf16[1,256,256]{2,1,0:T(8,128)(2,1)S(1)} custom-call(s32[1,4]{1,0:T(1,128)S(1)} %copy-done.3, bf16[1024,256]{1,0:T(8,128)(2,1)S(1)} %constant_dynamic-update-slice_fusion.8.q_ref, bf16[1024,128]{1,0:T(8,128)(2,1)S(1)} %get-tuple-element.44.refs_0_, bf16[1024,128]{1,0:T(8,128)(2,1)S(1)} %collective-permute-done.9.refs_1_, ...), custom_call_target="tpu_custom_call" | custom-call | flops 2147483648 | bytes 2097152 | tf_op jit(solution)/shard_map/pallas_call | solution.py:189
  60.4 0.6 collective-permute-start.17
  61.0 2.5 %shard_map.50 = bf16[1,256,256]{2,1,0:T(8,128)(2,1)S(1)} custom-call(s32[1,4]{1,0:T(1,128)S(1)} %copy-done.3, bf16[1024,256]{1,0:T(8,128)(2,1)S(1)} %constant_dynamic-update-slice_fusion.8.q_ref, bf16[1024,128]{1,0:T(8,128)(2,1)S(1)} %get-tuple-element.44.refs_0_, bf16[1024,128]{1,0:T(8,128)(2,1)S(1)} %collective-permute-done.9.refs_1_, ...), custom_call_target="tpu_custom_call" | custom-call | flops 2147483648 | bytes 2097152 | tf_op jit(solution)/shard_map/pallas_call | solution.py:189
  63.6 0.0 collective-permute-done.19.refs_3_
  63.6 5.3 %collective-permute-done.18.refs_2_ = bf16[256,256]{1,0:T(8,128)(2,1)S(1)} collective-permute-done((bf16[256,256]{1,0:T(8,128)(2,1)S(1)}, bf16[256,256]{1,0:T(8,128)(2,1)S(1)}, u32[]{:S(2)}, u32[]{:S(2)}) %collective-permute-start.18) | collective-permute-done | bytes 131104 | tf_op jit(solution)/shard_map/ppermute | solution.py:272
  68.9 0.0 collective-permute-done.17.refs_1_
  68.9 0.9 %shard_map.54 = bf16[256,1024]{1,0:T(8,128)(2,1)} custom-call(bf16[256,256]{1,0:T(8,128)(2,1)S(1)} %bitcast.4, bf16[256,256]{1,0:T(8,128)(2,1)S(1)} %collective-permute-done.17.refs_1_, bf16[256,256]{1,0:T(8,128)(2,1)S(1)} %collective-permute-done.18.refs_2_, bf16[256,256]{1,0:T(8,128)(2,1)S(1)} %collective-permute-done.19.refs_3_), custom_call_target="tpu_custom_call" | custom-call | tf_op jit(solution)/shard_map/pallas_call | solution.py:254
  (26 shorter events, 0.4 us)
Async XLA Ops:
  0.0 1.0 %copy-start = (bf16[256,1024]{1,0:T(8,128)(2,1)S(1)}, bf16[256,1024]{1,0:T(8,128)(2,1)}, u32[]{:S(2)}) copy-start(bf16[256,1024]{1,0:T(8,128)(2,1)} %refs_1_.1) | copy-start | bytes 1572868
  1.0 0.9 %copy-start.1 = (bf16[256,512]{1,0:T(8,128)(2,1)S(1)}, bf16[256,512]{1,0:T(8,128)(2,1)}, u32[]{:S(2)}) copy-start(bf16[256,512]{1,0:T(8,128)(2,1)} %refs_0_.2) | copy-start | bytes 786436
  2.0 7.3 %copy-start.2 = (bf16[256,512]{1,0:T(8,128)(2,1)S(1)}, bf16[256,512]{1,0:T(8,128)(2,1)}, u32[]{:S(2)}) copy-start(bf16[256,512]{1,0:T(8,128)(2,1)} %refs_0_.3) | copy-start | bytes 786436
  2.2 8.3 %collective-permute-start.10 = (bf16[256,128]{1,0:T(8,128)(2,1)S(1)}, bf16[256,128]{1,0:T(8,128)(2,1)S(1)}, u32[]{:S(2)}, u32[]{:S(2)}) collective-permute-start(bf16[256,128]{1,0:T(8,128)(2,1)S(1)} %get-tuple-element.32), channel_id=1, source_target_pairs={{0,1},{1,2},{2,3},{3,0},{4,5},{5,6},{6,7},{7,4},{8,9},{9,10},{10,1... | collective-permute-start | bytes 196616 | tf_op jit(solution)/shard_map/ppermute | solution.py:272
  5.3 8.1 %collective-permute-start.11 = (bf16[256,128]{1,0:T(8,128)(2,1)S(1)}, bf16[256,128]{1,0:T(8,128)(2,1)S(1)}, u32[]{:S(2)}, u32[]{:S(2)}) collective-permute-start(bf16[256,128]{1,0:T(8,128)(2,1)S(1)} %get-tuple-element.33), channel_id=1, source_target_pairs={{0,2},{1,3},{2,0},{3,1},{4,6},{5,7},{6,4},{7,5},{8,10},{9,11},{10,... | collective-permute-start | bytes 196616 | tf_op jit(solution)/shard_map/ppermute | solution.py:272
  7.9 5.6 %collective-permute-start.12 = (bf16[256,128]{1,0:T(8,128)(2,1)S(1)}, bf16[256,128]{1,0:T(8,128)(2,1)S(1)}, u32[]{:S(2)}, u32[]{:S(2)}) collective-permute-start(bf16[256,128]{1,0:T(8,128)(2,1)S(1)} %get-tuple-element.34), channel_id=1, source_target_pairs={{0,3},{1,0},{2,1},{3,2},{4,7},{5,4},{6,5},{7,6},{8,11},{9,8},{10,9... | collective-permute-start | bytes 196616 | tf_op jit(solution)/shard_map/ppermute | solution.py:272
  9.4 7.6 %collective-permute-start.3 = (bf16[256,128]{1,0:T(8,128)(2,1)S(1)}, bf16[256,128]{1,0:T(8,128)(2,1)S(1)}, u32[]{:S(2)}, u32[]{:S(2)}) collective-permute-start(bf16[256,128]{1,0:T(8,128)(2,1)S(1)} %get-tuple-element.28), channel_id=1, source_target_pairs={{0,1},{1,2},{2,3},{3,0},{4,5},{5,6},{6,7},{7,4},{8,9},{9,10},{10,1... | collective-permute-start | bytes 196616 | tf_op jit(solution)/shard_map/ppermute | solution.py:272
  10.1 7.9 %collective-permute-start.4 = (bf16[256,128]{1,0:T(8,128)(2,1)S(1)}, bf16[256,128]{1,0:T(8,128)(2,1)S(1)}, u32[]{:S(2)}, u32[]{:S(2)}) collective-permute-start(bf16[256,128]{1,0:T(8,128)(2,1)S(1)} %get-tuple-element.29), channel_id=1, source_target_pairs={{0,2},{1,3},{2,0},{3,1},{4,6},{5,7},{6,4},{7,5},{8,10},{9,11},{10,... | collective-permute-start | bytes 196616 | tf_op jit(solution)/shard_map/ppermute | solution.py:272
  10.6 7.5 %collective-permute-start.5 = (bf16[256,128]{1,0:T(8,128)(2,1)S(1)}, bf16[256,128]{1,0:T(8,128)(2,1)S(1)}, u32[]{:S(2)}, u32[]{:S(2)}) collective-permute-start(bf16[256,128]{1,0:T(8,128)(2,1)S(1)} %get-tuple-element.30), channel_id=1, source_target_pairs={{0,3},{1,0},{2,1},{3,2},{4,7},{5,4},{6,5},{7,6},{8,11},{9,8},{10,9... | collective-permute-start | bytes 196616 | tf_op jit(solution)/shard_map/ppermute | solution.py:272
  13.5 15.3 %collective-permute-start.13 = (bf16[1024,128]{1,0:T(8,128)(2,1)S(1)}, bf16[1024,128]{1,0:T(8,128)(2,1)S(1)}, u32[]{:S(2)}, u32[]{:S(2)}) collective-permute-start(bf16[1024,128]{1,0:T(8,128)(2,1)S(1)} %constant_dynamic-update-slice_fusion.refs_1_), channel_id=1, source_target_pairs={{0,16},{4,20},{8,24},{12,28},{1,17},{5,21},{9,25},{13,29},{2,18},{... | collective-permute-start | bytes 786440 | tf_op jit(solution)/shard_map/ppermute | solution.py:285
  18.1 19.1 %collective-permute-start.6 = (bf16[1024,128]{1,0:T(8,128)(2,1)S(1)}, bf16[1024,128]{1,0:T(8,128)(2,1)S(1)}, u32[]{:S(2)}, u32[]{:S(2)}) collective-permute-start(bf16[1024,128]{1,0:T(8,128)(2,1)S(1)} %constant_dynamic-update-slice_fusion.4.refs_0_), channel_id=1, source_target_pairs={{0,16},{4,20},{8,24},{12,28},{1,17},{5,21},{9,25},{13,29},{2,18},{... | collective-permute-start | bytes 786440 | tf_op jit(solution)/shard_map/ppermute | solution.py:285
  21.7 7.9 %collective-permute-start = (bf16[256,256]{1,0:T(8,128)(2,1)S(1)}, bf16[256,256]{1,0:T(8,128)(2,1)S(1)}, u32[]{:S(2)}, u32[]{:S(2)}) collective-permute-start(bf16[256,256]{1,0:T(8,128)(2,1)S(1)} %get-tuple-element.24), channel_id=1, source_target_pairs={{0,1},{1,2},{2,3},{3,0},{4,5},{5,6},{6,7},{7,4},{8,9},{9,10},{10,1... | collective-permute-start | bytes 393224 | tf_op jit(solution)/shard_map/ppermute | solution.py:272
  23.3 10.5 %collective-permute-start.1 = (bf16[256,256]{1,0:T(8,128)(2,1)S(1)}, bf16[256,256]{1,0:T(8,128)(2,1)S(1)}, u32[]{:S(2)}, u32[]{:S(2)}) collective-permute-start(bf16[256,256]{1,0:T(8,128)(2,1)S(1)} %get-tuple-element.25), channel_id=1, source_target_pairs={{0,2},{1,3},{2,0},{3,1},{4,6},{5,7},{6,4},{7,5},{8,10},{9,11},{10,... | collective-permute-start | bytes 393224 | tf_op jit(solution)/shard_map/ppermute | solution.py:272
  25.4 12.5 %collective-permute-start.15 = (bf16[1024,128]{1,0:T(8,128)(2,1)S(1)}, bf16[1024,128]{1,0:T(8,128)(2,1)S(1)}, u32[]{:S(2)}, u32[]{:S(2)}) collective-permute-start(bf16[1024,128]{1,0:T(8,128)(2,1)S(1)} %constant_dynamic-update-slice_fusion.refs_1_), channel_id=1, source_target_pairs={{0,8},{4,12},{8,16},{16,24},{20,28},{1,9},{5,13},{9,17},{17,25},{2... | collective-permute-start | bytes 786440 | tf_op jit(solution)/shard_map/ppermute | solution.py:285
  28.8 9.1 %collective-permute-start.14 = (bf16[1024,128]{1,0:T(8,128)(2,1)S(1)}, bf16[1024,128]{1,0:T(8,128)(2,1)S(1)}, u32[]{:S(2)}, u32[]{:S(2)}) collective-permute-start(bf16[1024,128]{1,0:T(8,128)(2,1)S(1)} %collective-permute-done.13.refs_1_), channel_id=1, source_target_pairs={{28,20},{29,21},{30,22},{31,23}} | collective-permute-start | bytes 786440 | tf_op jit(solution)/shard_map/ppermute | solution.py:285
  29.6 13.4 %collective-permute-start.2 = (bf16[256,256]{1,0:T(8,128)(2,1)S(1)}, bf16[256,256]{1,0:T(8,128)(2,1)S(1)}, u32[]{:S(2)}, u32[]{:S(2)}) collective-permute-start(bf16[256,256]{1,0:T(8,128)(2,1)S(1)} %get-tuple-element.26), channel_id=1, source_target_pairs={{0,3},{1,0},{2,1},{3,2},{4,7},{5,4},{6,5},{7,6},{8,11},{9,8},{10,9... | collective-permute-start | bytes 393224 | tf_op jit(solution)/shard_map/ppermute | solution.py:272
  33.8 9.0 %collective-permute-start.8 = (bf16[1024,128]{1,0:T(8,128)(2,1)S(1)}, bf16[1024,128]{1,0:T(8,128)(2,1)S(1)}, u32[]{:S(2)}, u32[]{:S(2)}) collective-permute-start(bf16[1024,128]{1,0:T(8,128)(2,1)S(1)} %constant_dynamic-update-slice_fusion.4.refs_0_), channel_id=1, source_target_pairs={{0,8},{4,12},{8,16},{16,24},{20,28},{1,9},{5,13},{9,17},{17,25},{2... | collective-permute-start | bytes 786440 | tf_op jit(solution)/shard_map/ppermute | solution.py:285
  37.2 5.6 %collective-permute-start.7 = (bf16[1024,128]{1,0:T(8,128)(2,1)S(1)}, bf16[1024,128]{1,0:T(8,128)(2,1)S(1)}, u32[]{:S(2)}, u32[]{:S(2)}) collective-permute-start(bf16[1024,128]{1,0:T(8,128)(2,1)S(1)} %collective-permute-done.6.refs_0_), channel_id=1, source_target_pairs={{28,20},{29,21},{30,22},{31,23}} | collective-permute-start | bytes 786440 | tf_op jit(solution)/shard_map/ppermute | solution.py:285
  38.0 12.5 %collective-permute-start.16 = (bf16[1024,128]{1,0:T(8,128)(2,1)S(1)}, bf16[1024,128]{1,0:T(8,128)(2,1)S(1)}, u32[]{:S(2)}, u32[]{:S(2)}) collective-permute-start(bf16[1024,128]{1,0:T(8,128)(2,1)S(1)} %get-tuple-element.41), channel_id=1, source_target_pairs={{0,4},{4,0},{8,12},{12,8},{16,20},{20,16},{24,28},{28,24},{1,5},{5... | collective-permute-start | bytes 786440 | tf_op jit(solution)/shard_map/ppermute | solution.py:285
  42.9 0.7 copy-start.3
  42.9 7.6 %collective-permute-start.9 = (bf16[1024,128]{1,0:T(8,128)(2,1)S(1)}, bf16[1024,128]{1,0:T(8,128)(2,1)S(1)}, u32[]{:S(2)}, u32[]{:S(2)}) collective-permute-start(bf16[1024,128]{1,0:T(8,128)(2,1)S(1)} %get-tuple-element.43), channel_id=1, source_target_pairs={{0,4},{4,0},{8,12},{12,8},{16,20},{20,16},{24,28},{28,24},{1,5},{5... | collective-permute-start | bytes 786440 | tf_op jit(solution)/shard_map/ppermute | solution.py:285
  53.0 10.6 %collective-permute-start.19 = (bf16[256,256]{1,0:T(8,128)(2,1)S(1)}, bf16[256,256]{1,0:T(8,128)(2,1)S(1)}, u32[]{:S(2)}, u32[]{:S(2)}) collective-permute-start(bf16[256,256]{1,0:T(8,128)(2,1)S(1)} %bitcast.5), channel_id=1, source_target_pairs={{0,3},{1,0},{2,1},{3,2},{4,7},{5,4},{6,5},{7,6},{8,11},{9,8},{10,9... | collective-permute-start | bytes 393224 | tf_op jit(solution)/shard_map/ppermute | solution.py:272
  57.8 11.1 %collective-permute-start.18 = (bf16[256,256]{1,0:T(8,128)(2,1)S(1)}, bf16[256,256]{1,0:T(8,128)(2,1)S(1)}, u32[]{:S(2)}, u32[]{:S(2)}) collective-permute-start(bf16[256,256]{1,0:T(8,128)(2,1)S(1)} %bitcast.6), channel_id=1, source_target_pairs={{0,2},{1,3},{2,0},{3,1},{4,6},{5,7},{6,4},{7,5},{8,10},{9,11},{10,... | collective-permute-start | bytes 393224 | tf_op jit(solution)/shard_map/ppermute | solution.py:272
  60.4 8.5 %collective-permute-start.17 = (bf16[256,256]{1,0:T(8,128)(2,1)S(1)}, bf16[256,256]{1,0:T(8,128)(2,1)S(1)}, u32[]{:S(2)}, u32[]{:S(2)}) collective-permute-start(bf16[256,256]{1,0:T(8,128)(2,1)S(1)} %bitcast.7), channel_id=1, source_target_pairs={{0,1},{1,2},{2,3},{3,0},{4,5},{5,6},{6,7},{7,4},{8,9},{9,10},{10,1... | collective-permute-start | bytes 393224 | tf_op jit(solution)/shard_map/ppermute | solution.py:272
